TPU v7x, 256 devices: a whole 4x4x8 slice. The times are simulated.
256 devices in a mesh: sens: 4 (over y), samp: 64 (over z, x, core).
Axes of the slice: x: 4, y: 4, z: 8, core: 2. Of those that a mesh axis runs over, the one named last changes fastest.
Arguments:
- slopes: bfloat16 [2, 256, 150528], P(None, 'samp', 'sens'), may hold values from -0.0625 to 0.0625
- targets: bfloat16 [2, 16384, 256], P(None, 'samp'), may hold values from -6 to 6
- reconstructor: float32 [4, 64, 32, 128, 128], P('sens', 'samp'), may hold values from -6 to 6
- foot_act: int32 [4, 64, 32], P('sens'), may hold values from 0 to 1, as said below
- foot_slope: int32 [4, 64, 32], P('sens'), may hold values from 0 to 293, as said below
- foot_count: int32 [4, 64], P('sens'), may hold values from 16 to 32, as said below
Outputs:
- fitted: float32 [4, 64, 32, 128, 128], P('sens', 'samp')
- fit_residual: bfloat16 [16384, 256], P('samp')
Inputs may be any that keep to these rules, and one draw needn't show every extreme that they name: `foot_act`: slots 0 to foot_count-1 of a device are live, the rest padding (actuator block 0 and a slope block already named by slot 0); no (actuator block, slope block) pair repeats among live slots; the slope blocks of one actuator block form a run of consecutive blocks modulo 294. `foot_slope`: the live slots of one device name at most 20 distinct slope blocks; for every sens index some device names exactly 20. `foot_count`: for every sens index some device has 32 live slots.
All inputs are finite; a program needn't handle non-finite values.
Results may differ from a plain program's by a relative error of at most 0.0037.
Values may be sent and summed in bfloat16 or wider, within the bound.
A program may use at most 64 MiB of HBM per device.

v0:
```python
import jax
import jax.numpy as jnp
from jax import lax
from jax.sharding import PartitionSpec as P

STEPS = 2


def per_device(slopes, targets, reconstructor, foot_act, foot_slope, foot_count):
    samp_count = lax.axis_size("samp")
    own_index = lax.axis_index("samp")
    block_size = reconstructor.shape[-1]
    slot_count = reconstructor.shape[2]
    groups = slopes.shape[2] // block_size
    samp_dev = slopes.shape[1]
    act_blocks = targets.shape[1] // block_size
    samples = targets.shape[2]
    step_rate = slot_count * block_size / (samples + 3 * slot_count * block_size)
    act_all = foot_act[0]
    slope_all = foot_slope[0]
    count_all = foot_count[0]
    live_all = jnp.arange(slot_count)[None, :] < count_all[:, None]
    own_act = lax.dynamic_index_in_dim(act_all, own_index, 0, keepdims=False)
    own_live = lax.dynamic_index_in_dim(live_all, own_index, 0, keepdims=False)
    act_onehot = ((own_act[None, :] == jnp.arange(act_blocks)[:, None]) & own_live[None, :]).astype(
        jnp.float32
    )
    need_count = slope_all.shape[1]
    weights = reconstructor[0, 0]
    fit_residual = None
    for step in range(STEPS):
        local_rows = slopes[step].reshape(samp_dev, groups, block_size)
        outgoing = jnp.take(local_rows, slope_all.reshape(-1), axis=1)
        outgoing = outgoing.reshape(samp_dev, samp_count, need_count, block_size)
        arrived = lax.all_to_all(outgoing, "samp", split_axis=1, concat_axis=0, tiled=True)
        slot_slopes = arrived.reshape(samples, need_count, block_size)
        weights_low = weights.astype(jnp.bfloat16)
        partial_sums = jnp.einsum(
            "kil,nkl->kin", weights_low, slot_slopes, preferred_element_type=jnp.float32
        )
        summed = jnp.einsum(
            "jk,kin->jin", act_onehot, partial_sums, precision=lax.Precision.HIGHEST
        )
        target_now = targets[step].reshape(act_blocks, block_size, samples)
        total = lax.psum(summed, "sens")
        residual = (total - target_now).astype(jnp.bfloat16)
        slot_residual = jnp.take(residual, own_act, axis=0)
        gradient = jnp.einsum(
            "kin,nkl->kil", slot_residual, slot_slopes, preferred_element_type=jnp.float32
        )
        weights = jnp.where(own_live[:, None, None], weights - step_rate * gradient, weights)
        fit_residual = residual
    return (weights[None, None], fit_residual.reshape(act_blocks * block_size, samples))


def solution(mesh):
    return jax.shard_map(
        per_device,
        mesh=mesh,
        in_specs=(
            P(None, "samp", "sens"),
            P(None, "samp", None),
            P("sens", "samp", None, None, None),
            P("sens", None, None),
            P("sens", None, None),
            P("sens", None),
        ),
        out_specs=(P("sens", "samp", None, None, None), P("samp", None)),
        check_vma=False,
    )
```

profile of v0, /device:TPU:1, one launch (start us, length us, event | category | flops | bytes accessed | tf_op | source)
XLA Modules:
  0.0 258.7 jit_solution(15203739831678689904)
XLA Ops:
  7.2 0.0 copy-start
  7.2 0.8 copy.50
  8.0 0.1 reshape_squeeze.13
  8.1 1.3 slice_bitcast_fusion
  9.4 14.6 %gather_fusion.2 = bf16[2048,4,128]{2,1,0:T(4,128)(2,1)} fusion(bf16[4,294,128]{2,0,1:T(4,128)(2,1)S(1)} %get-tuple-element.4, s32[2048]{0:T(1024)S(1)} %fusion.19), kind=kCustom, calls=%fused_computation.2.clone | custom fusion | bytes 4202496 | tf_op jit(solution)/shard_map/jit(_take)/gather | solution.py:33
  24.0 14.5 %gather_fusion = bf16[2048,4,128]{2,1,0:T(4,128)(2,1)} fusion(bf16[4,294,128]{2,0,1:T(4,128)(2,1)S(1)} %get-tuple-element.5, s32[2048]{0:T(1024)S(1)} %fusion.19), kind=kCustom, calls=%fused_computation.clone | custom fusion | bytes 4202496 | tf_op jit(solution)/shard_map/jit(_take)/gather | solution.py:33
  38.5 10.6 %broadcast_select_fusion = (bf16[2048,4,128]{2,1,0:T(4,128)(2,1)S(1)}, bf16[2048,4,128]{2,1,0:T(4,128)(2,1)S(1)}) fusion(bf16[2048,4,128]{2,1,0:T(4,128)(2,1)} %gather_fusion.2, pred[2048]{0:T(1024)(128)(4,1)S(1)} %compare_and_fusion, bf16[2048,4,128]{2,1,0:T(4,128)(2,1)} %gather_fusion), kind=kLoop, calls=%fused_computation.15 | loop fusion | flops 2097152 | bytes 8390656 | tf_op jit(solution)/shard_map/jit(_take)/select_n | solution.py:33
  49.0 1.9 copy.53
  50.9 13.2 %all-to-all-start = ((bf16[4,64,32,128]{3,2,0,1:T(8,128)(2,1)}), bf16[4,64,32,128]{3,2,0,1:T(8,128)(2,1)}, u32[]{:S(2)}, u32[]{:S(2)}) async-start(bf16[4,64,32,128]{3,2,0,1:T(8,128)(2,1)} %copy.53), calls=%async_computation | async-start | bytes 4194304 | tf_op jit(solution)/shard_map/all_to_all | solution.py:35
  64.1 1.9 copy.59
  66.1 0.0 copy-start.6
  66.1 47.6 %all-to-all-done = bf16[4,64,32,128]{3,2,0,1:T(8,128)(2,1)} async-done(((bf16[4,64,32,128]{3,2,0,1:T(8,128)(2,1)}), bf16[4,64,32,128]{3,2,0,1:T(8,128)(2,1)}, u32[]{:S(2)}, u32[]{:S(2)}) %all-to-all-start) | async-done | bytes 2097184 | tf_op jit(solution)/shard_map/all_to_all | solution.py:35
  113.7 7.0 %all-to-all-start.1 = ((bf16[4,64,32,128]{3,2,0,1:T(8,128)(2,1)}), bf16[4,64,32,128]{3,2,0,1:T(8,128)(2,1)S(1)}, u32[]{:S(2)}, u32[]{:S(2)}) async-start(bf16[4,64,32,128]{3,2,0,1:T(8,128)(2,1)} %copy.59), calls=%async_computation.1 | async-start | bytes 4194304 | tf_op jit(solution)/shard_map/all_to_all | solution.py:35
  120.7 0.0 all-reduce.3.cloned.1.call-start
  120.8 0.0 copy-done.6
  120.8 0.6 dynamic-slice.1
  121.4 0.0 copy-done
  121.4 0.2 dynamic-slice_reduce_fusion
  121.6 0.7 compare_bitcast_fusion
  122.3 0.0 copy-start.4
  122.3 2.8 %copy.54 = bf16[64,4,1,32,128]{4,1,0,3,2:T(4,128)(2,1)S(1)} copy(bf16[64,4,1,32,128]{4,3,1,0,2:T(8,128)(2,1)} %bitcast.8) | data formatting | bytes 4194304 | tf_op jit(solution)/shard_map/all_to_all | solution.py:35
  125.1 0.0 copy-start.2
  125.1 1.3 copy-done.2
  126.4 0.0 copy-done.4
  126.4 2.7 %convolution_bitcast_fusion = f32[32,128,256]{1,2,0:T(8,128)} fusion(bf16[256,32,128]{2,0,1:T(8,128)(2,1)S(1)} %bitcast.54, f32[1,1,32,128,128]{4,3,2,1,0:T(8,128)S(1)} %copy-done.4), kind=kOutput, calls=%fused_computation.8 | convolution fusion | flops 268435456 | bytes 8388608 | tf_op jit(solution)/shard_map/kil,nkl->kin/dot_general | solution.py:38
  129.1 5.5 %copy.55 = f32[32,128,256]{2,0,1:T(8,128)} copy(f32[32,128,256]{1,2,0:T(8,128)} %convolution_bitcast_fusion) | data formatting | bytes 8388608 | tf_op jit(solution)/shard_map/kil,nkl->kin/dot_general | solution.py:38
  134.6 3.7 %fusion.21 = f32[2,128,256]{2,0,1:T(2,128)S(1)} fusion(f32[32,128,256]{2,0,1:T(8,128)} %copy.55, pred[32]{0:T(512)(128)(4,1)S(1)} %compare_bitcast_fusion, s32[32]{0:T(128)S(1)} %dynamic-slice_reduce_fusion), kind=kOutput, calls=%fused_computation.36 | convolution fusion | flops 25165952 | bytes 4456608 | tf_op jit(solution)/shard_map/jk,kin->jin/dot_general | solution.py:41
  138.3 0.7 copy.56
  139.0 0.0 all-reduce.3.cloned.1.call-update
  139.0 0.2 all-reduce.5.cloned.1.call-start
  139.2 0.0 copy-done.5
  139.3 31.1 %all-to-all-done.1 = bf16[4,64,32,128]{3,2,0,1:T(8,128)(2,1)S(1)} async-done(((bf16[4,64,32,128]{3,2,0,1:T(8,128)(2,1)}), bf16[4,64,32,128]{3,2,0,1:T(8,128)(2,1)S(1)}, u32[]{:S(2)}, u32[]{:S(2)}) %all-to-all-start.1) | async-done | bytes 2097184 | tf_op jit(solution)/shard_map/all_to_all | solution.py:35
  170.4 2.4 copy.60
  172.8 12.1 %all-reduce.3.cloned.1.call-done = f32[2,128,256]{2,1,0:T(8,128)} async-done(((f32[2,128,256]{2,1,0:T(8,128)}), f32[2,128,256]{2,1,0:T(8,128)}) %all-reduce.3.cloned.1.call-update) | async-done | bytes 262160 | tf_op jit(solution)/shard_map/psum | solution.py:45
  184.9 1.0 fusion.18
  185.9 2.0 gather_fusion.1
  187.9 3.8 %subtract_select_fusion.1 = f32[32,128,128]{2,1,0:T(8,128)S(1)} fusion(f32[1,1,32,128,128]{4,3,2,1,0:T(8,128)} %param.12, bf16[256,32,128]{2,0,1:T(8,128)(2,1)} %bitcast.55, bf16[32,128,256]{2,1,0:T(8,128)(2,1)} %gather_fusion.1, pred[32]{0:T(512)(128)(4,1)S(1)} %compare_and_fusion.1, pred[32]{0:T(512)(128)(4,1)S(1)} %compare_bitcast_fusion), kind=kOutput, calls=%fused_computation.7 | convolution fusion | flops 271056896 | bytes 8388672 | tf_op jit(solution)/shard_map/kin,nkl->kil/dot_general | solution.py:48
  191.8 0.0 copy-done.3
  191.8 0.7 fusion.15
  192.5 3.8 %fusion = f32[2,128,256]{2,0,1:T(2,128)S(1)} fusion(f32[32,128,256]{2,1,0:T(8,128)S(1)} %fusion.15, pred[32]{0:T(512)(128)(4,1)S(1)} %compare_bitcast_fusion, s32[32]{0:T(128)S(1)} %dynamic-slice_reduce_fusion), kind=kOutput, calls=%fused_computation.4 | convolution fusion | flops 25165952 | bytes 4456608 | tf_op jit(solution)/shard_map/jk,kin->jin/dot_general | solution.py:41
  196.3 0.7 copy.62
  197.0 0.0 all-reduce.5.cloned.1.call-update
  197.1 47.4 %all-reduce.5.cloned.1.call-done = f32[2,128,256]{2,1,0:T(8,128)} async-done(((f32[2,128,256]{2,1,0:T(8,128)}), f32[2,128,256]{2,1,0:T(8,128)}) %all-reduce.5.cloned.1.call-update) | async-done | bytes 262160 | tf_op jit(solution)/shard_map/psum | solution.py:45
  244.5 1.0 fusion.17
  245.5 0.0 copy-start.1
  245.5 2.0 gather_fusion.3
  247.5 0.0 copy-done.1
  247.5 4.4 %fusion.2 = f32[1,1,32,128,128]{4,3,2,1,0:T(8,128)} fusion(f32[32,128,128]{2,1,0:T(8,128)S(1)} %subtract_select_fusion.1, bf16[256,32,128]{2,0,1:T(8,128)(2,1)} %bitcast.56, bf16[32,128,256]{2,1,0:T(8,128)(2,1)} %gather_fusion.3, pred[32]{0:T(512)(128)(4,1)S(1)} %compare_and_fusion.1, pred[32]{0:T(512)(128)(4,1)S(1)} %compare_bitcast_fusion), kind=kOutput, calls=%fused_computation.9 | convolution fusion | flops 271056896 | bytes 8388672 | tf_op jit(solution)/shard_map/kin,nkl->kil/dot_general | solution.py:48
  (8 shorter events, 0.1 us)
Async XLA Ops:
  7.2 114.2 %copy-start = (s32[1,64,32]{1,2,0:T(8,128)S(1)}, s32[1,64,32]{1,2,0:T(8,128)}, u32[]{:S(2)}) copy-start(s32[1,64,32]{1,2,0:T(8,128)} %param.13) | copy-start | bytes 24580
  50.9 62.8 %all-to-all-start = ((bf16[4,64,32,128]{3,2,0,1:T(8,128)(2,1)}), bf16[4,64,32,128]{3,2,0,1:T(8,128)(2,1)}, u32[]{:S(2)}, u32[]{:S(2)}) async-start(bf16[4,64,32,128]{3,2,0,1:T(8,128)(2,1)} %copy.53), calls=%async_computation | async-start | bytes 4194304 | tf_op jit(solution)/shard_map/all_to_all | solution.py:35
  66.1 54.7 %copy-start.6 = (s32[1,64]{1,0:T(1,128)S(1)}, s32[1,64]{1,0:T(1,128)}, u32[]{:S(2)}) copy-start(s32[1,64]{1,0:T(1,128)} %param.15) | copy-start | bytes 772
  113.7 56.7 %all-to-all-start.1 = ((bf16[4,64,32,128]{3,2,0,1:T(8,128)(2,1)}), bf16[4,64,32,128]{3,2,0,1:T(8,128)(2,1)S(1)}, u32[]{:S(2)}, u32[]{:S(2)}) async-start(bf16[4,64,32,128]{3,2,0,1:T(8,128)(2,1)} %copy.59), calls=%async_computation.1 | async-start | bytes 4194304 | tf_op jit(solution)/shard_map/all_to_all | solution.py:35
  120.7 64.2 %all-reduce.3.cloned.1.call-start = ((), (), s32[]{:S(2)}) async-start(), calls=%async_computation.2 | async-start | bytes 524288 | tf_op jit(solution)/shard_map/psum | solution.py:45
  122.3 4.2 %copy-start.4 = (f32[1,1,32,128,128]{4,3,2,1,0:T(8,128)S(1)}, f32[1,1,32,128,128]{4,3,2,1,0:T(8,128)}, u32[]{:S(2)}) copy-start(f32[1,1,32,128,128]{4,3,2,1,0:T(8,128)} %param.12) | copy-start | bytes 6291460
  125.1 1.3 copy-start.2
  134.6 4.7 %copy-start.5 = (bf16[2,256,256]{2,1,0:T(8,128)(2,1)S(1)}, bf16[2,256,256]{2,1,0:T(8,128)(2,1)}, u32[]{:S(2)}) copy-start(bf16[2,256,256]{2,1,0:T(8,128)(2,1)} %param.11) | copy-start | bytes 786436
  139.0 105.5 %all-reduce.5.cloned.1.call-start = ((), (), s32[]{:S(2)}) async-start(), calls=%async_computation.3 | async-start | bytes 524288 | tf_op jit(solution)/shard_map/psum | solution.py:45
  187.9 3.9 %copy-start.3 = (bf16[64,4,1,32,128]{4,1,0,3,2:T(4,128)(2,1)S(1)}, bf16[64,4,1,32,128]{4,1,0,3,2:T(4,128)(2,1)}, u32[]{:S(2)}) copy-start(bf16[64,4,1,32,128]{4,1,0,3,2:T(4,128)(2,1)} %copy.60) | copy-start | bytes 6291460
  245.5 2.0 copy-start.1
Sparse Core Ops, SparseCore 0:
  139.1 45.7 all-reduce.2
  197.2 47.2 all-reduce.4
where the time goes:
time: 261 us; the launch traced here: 259 us
  waiting for transfers between devices  138 us (53%)
  local copies, waits for them, and re-layouts  53.4 us (20%)
  starting transfers between devices  20.5 us (8%)
  matrix products  19.1 us (7%)
  between operations  14.2 us (5%)
  other arithmetic  13.2 us (5%)
    all_to_all x2, waiting for transfers between devices, per_device(): lax.all_to_all(outgoing, 'samp', split_axis=1, concat_axis=0, tiled=True)  78.8 us
    psum x2, waiting for transfers between devices, per_device(): total = lax.psum(summed, 'sens')  59.5 us
    gather x2, local copies, waits for them, and re-layouts, per_device(): outgoing = jnp.take(local_rows, slope_all.reshape(-1), axis=1)  29.1 us
    all_to_all x2, starting transfers between devices, per_device(): lax.all_to_all(outgoing, 'samp', split_axis=1, concat_axis=0, tiled=True)  20.2 us
    select_n x1, other arithmetic, per_device(): outgoing = jnp.take(local_rows, slope_all.reshape(-1), axis=1)  10.6 us
    dot_general x2, matrix products, per_device(): jnp.einsum('kin,nkl->kil', slot_residual, slot_slopes, preferred_element_...  8.22 us
    dot_general x2, matrix products, per_device(): jnp.einsum('jk,kin->jin', act_onehot, partial_sums, precision=lax.Precisi...  7.5 us
    dot_general x1, local copies, waits for them, and re-layouts, per_device(): jnp.einsum('kil,nkl->kin', weights_low, slot_slopes, preferred_element_ty...  5.48 us
  transfers between devices with their start and end apart: 4, of which 4 were waited for; matrix products, arithmetic and copies ran while one was open for 8% of the time, Pallas kernels for 0%

commit v1 on v0

v1 whole, which is shorter than its diff:
```python
import functools

import jax
import jax.numpy as jnp
from jax import lax
from jax.experimental import pallas as pl
from jax.experimental.pallas import tpu as pltpu
from jax.sharding import PartitionSpec as P

MESH = pl.DeviceIdType.MESH
STEPS = 2
SB = 128
SGB = 294
K_MAX = 32
DIST = 20
ACT_DEV = 2
SAMPLES = 256
LOCAL = 4
WIDE = DIST * SB
HALF = SGB // 2
RATE = K_MAX * SB / (SAMPLES + 3 * K_MAX * SB)
OFFS = (0, -1, 1, -2, 2, -3, 3, 4)
F32 = jnp.float32
BF16 = jnp.bfloat16


def place(off):
    return OFFS.index(4 if off == -4 else off)


def kernel(slopes, targets, recon, dist_tab, int_tab, flt_tab, fitted, resid_out,
           grid0, grid1, pick0, pick1, got0, got1, mat, weights, low_t, recon_v, outbuf,
           preds, goal, perm, load_sem, zs, zr, xs, xr, ys, yr, out_sem):
    grids, picks, gots = (grid0, grid1), (pick0, pick1), (got0, got1)
    sens = lax.axis_index("sens")
    samp = lax.axis_index("samp")
    plane = samp // 8
    col = (samp % 8) // 2
    core = samp % 2
    own_q = samp % 8

    def z_dev(step):
        return (sens, (samp + 8 * step + 64) % 64)

    def q_of(e, sign):
        return ((col + sign * (e // 2) + 4) % 4) * 2 + (core + e) % 2

    def z_copy(way, t, hop, half):
        sign = -1 if way == 0 else 1
        window = pl.ds(half * HALF, HALF)
        return pltpu.make_async_remote_copy(
            src_ref=grids[t][place(sign * hop)].at[window],
            dst_ref=grids[t][place(sign * (hop + 1))].at[window],
            send_sem=zs.at[way, t, hop, half],
            recv_sem=zr.at[way, t, hop, half],
            device_id=z_dev(-sign),
            device_id_type=MESH,
        )

    def x_copy(t, r, e):
        return pltpu.make_async_remote_copy(
            src_ref=picks[t][r].at[e],
            dst_ref=gots[t].at[r, own_q],
            send_sem=xs.at[t, r, e],
            recv_sem=xr.at[t, r, e],
            device_id=(sens, plane * 8 + q_of(e, 1)),
            device_id_type=MESH,
        )

    def x_arrival(t, r, e):
        return pltpu.make_async_remote_copy(
            src_ref=picks[t][r].at[e],
            dst_ref=gots[t].at[r, q_of(e, -1)],
            send_sem=xs.at[t, r, e],
            recv_sem=xr.at[t, r, e],
            device_id=(sens, plane * 8 + q_of(e, -1)),
            device_id_type=MESH,
        )

    def y_copy(t, e):
        return pltpu.make_async_remote_copy(
            src_ref=preds.at[t, sens],
            dst_ref=preds.at[t, sens],
            send_sem=ys.at[t, e - 1],
            recv_sem=yr.at[t, e - 1],
            device_id=((sens + e) % 4, samp),
            device_id_type=MESH,
        )

    def y_arrival(t, e):
        other = (sens - e + 4) % 4
        return pltpu.make_async_remote_copy(
            src_ref=preds.at[t, other],
            dst_ref=preds.at[t, other],
            send_sem=ys.at[t, e - 1],
            recv_sem=yr.at[t, e - 1],
            device_id=(other, samp),
            device_id_type=MESH,
        )

    def forward(t, hop, half):
        for way in range(2):
            z_copy(way, t, hop - 1, half).wait_recv()
            if hop < 3 or half == way:
                z_copy(way, t, hop, half).start()

    def pick(t, r):
        src = grids[t][r]

        def one(e, to):
            row = plane * 8 + q_of(e, 1)
            for d in range(DIST):
                to[:, d * SB:(d + 1) * SB] = src[dist_tab[row, d]]

        one(0, gots[t].at[r, own_q])

        @pl.loop(1, 8)
        def _(e):
            one(e, picks[t][r].at[e])

    def send_picked(t, r):
        for e in range(1, 8):
            x_copy(t, r, e).start()

    def assemble(t, r):
        for e in range(1, 8):
            x_arrival(t, r, e).wait_recv()
        for half in range(2):
            piece = jnp.concatenate([gots[t][r, half * 4 + q] for q in range(4)], axis=0)
            mat[t, pl.ds(r * 32 + half * 16, 16), :] = piece

    def low_weights():
        @pl.loop(0, DIST)
        def _(d):
            for j in range(ACT_DEV):
                block = weights[j * DIST + d].astype(BF16)
                low_t[pl.ds(pl.multiple_of(d * SB, SB), SB), j * SB:(j + 1) * SB] = block.T

    def predict(t):
        part = jnp.dot(mat[t], low_t[...], preferred_element_type=F32)
        preds[t, sens] = part.astype(BF16)

    def residual(t):
        total = preds[t, 0].astype(F32)
        for s in range(1, 4):
            total = total + preds[t, s].astype(F32)
        return (total - goal[t]).astype(BF16).T

    def gradient(t, resid):
        @pl.loop(0, DIST // 2)
        def _(g):
            cols = pl.ds(pl.multiple_of(g * 2 * SB, 2 * SB), 2 * SB)
            grad = jnp.dot(resid, mat[t, :, cols], preferred_element_type=F32)
            for j in range(ACT_DEV):
                for side in range(2):
                    at = j * DIST + g * 2 + side
                    scale = RATE * flt_tab[at]
                    weights[at] = weights[at] - scale * grad[j * SB:(j + 1) * SB, side * SB:(side + 1) * SB]

    own_loads = [pltpu.make_async_copy(slopes.at[t], grids[t][0], load_sem.at[t]) for t in range(STEPS)]
    recon_load = pltpu.make_async_copy(recon, recon_v, load_sem.at[2])
    for load in own_loads:
        load.start()
    recon_load.start()

    barrier = pltpu.get_barrier_semaphore()
    for step in (1, -1):
        pl.semaphore_signal(barrier, inc=1, device_id=z_dev(step), device_id_type=MESH)
    for e in range(1, 8):
        pl.semaphore_signal(barrier, inc=1, device_id=(sens, plane * 8 + q_of(e, 1)), device_id_type=MESH)
    for e in range(1, 4):
        pl.semaphore_signal(barrier, inc=1, device_id=((sens + e) % 4, samp), device_id_type=MESH)
    pl.semaphore_wait(barrier, 12)

    own_loads[0].wait()
    for half in range(2):
        for way in range(2):
            z_copy(way, 0, 0, half).start()
    own_loads[1].wait()
    pick(0, 0)
    send_picked(0, 0)

    recon_load.wait()

    @pl.loop(0, ACT_DEV * DIST)
    def _(at):
        weights[at] = recon_v[int_tab[at]] * flt_tab[at]

    low_weights()

    rows = lax.broadcasted_iota(jnp.int32, (SAMPLES, SAMPLES), 0)
    cols = lax.broadcasted_iota(jnp.int32, (SAMPLES, SAMPLES), 1)
    off = jnp.zeros_like(rows)
    for r in range(8):
        off = jnp.where(rows // 32 == r, (plane + OFFS[r] + 8) % 8, off)
    perm[...] = jnp.where(cols == off * 32 + rows % 32, 1.0, 0.0).astype(BF16)
    for t in range(STEPS):
        goal[t] = lax.dot_general(perm[...], targets[t], (((1,), (1,)), ((), ())),
                                  preferred_element_type=F32)

    for hop in range(1, 4):
        for half in range(2):
            forward(0, hop, half)
        if hop == 3:
            for half in range(2):
                for way in range(2):
                    z_copy(way, 1, 0, half).start()
        for sign in (-1, 1):
            pick(0, place(sign * hop))
            send_picked(0, place(sign * hop))
        if hop > 1:
            for r in ((0, 1, 2) if hop == 2 else (3, 4)):
                assemble(0, r)
    pick(1, 0)
    send_picked(1, 0)
    for way in range(2):
        z_copy(way, 0, 3, way).wait_recv()
    pick(0, 7)
    send_picked(0, 7)
    assemble(0, 5)
    assemble(0, 6)
    forward(1, 1, 0)
    assemble(0, 7)
    predict(0)
    for e in range(1, 4):
        y_copy(0, e).start()
    forward(1, 1, 1)
    for r in (1, 2):
        pick(1, r)
        send_picked(1, r)
    assemble(1, 0)
    for e in range(1, 4):
        y_arrival(0, e).wait_recv()
    gradient(0, residual(0))
    forward(1, 2, 0)
    low_weights()
    forward(1, 2, 1)
    for r in (3, 4):
        pick(1, r)
        send_picked(1, r)
    assemble(1, 1)
    assemble(1, 2)
    for half in range(2):
        forward(1, 3, half)
    for r in (5, 6):
        pick(1, r)
        send_picked(1, r)
    assemble(1, 3)
    assemble(1, 4)
    for way in range(2):
        z_copy(way, 1, 3, way).wait_recv()
    pick(1, 7)
    send_picked(1, 7)
    for r in (5, 6, 7):
        assemble(1, r)
    predict(1)
    for e in range(1, 4):
        y_copy(1, e).start()
    for e in range(1, 4):
        y_arrival(1, e).wait_recv()
    resid = residual(1)
    gradient(1, resid)

    outs = []
    for c in range(4):
        @pl.loop(c * 8, (c + 1) * 8)
        def _(k):
            fresh = weights[int_tab[ACT_DEV * DIST + k]]
            live = flt_tab[ACT_DEV * DIST + k]
            outbuf[k] = fresh * live + recon_v[k] * (1.0 - live)

        out = pltpu.make_async_copy(outbuf.at[pl.ds(c * 8, 8)], fitted.at[pl.ds(c * 8, 8)], out_sem.at[c])
        out.start()
        outs.append(out)
    resid_out[...] = jnp.dot(resid, perm[...], preferred_element_type=F32).astype(BF16)

    for t in range(STEPS):
        for hop in range(4):
            for half in range(2):
                for way in range(2):
                    if hop < 3 or half == way:
                        z_copy(way, t, hop, half).wait_send()
        for r in range(8):
            for e in range(1, 8):
                x_copy(t, r, e).wait_send()
        for e in range(1, 4):
            y_copy(t, e).wait_send()
    for out in outs:
        out.wait()


def tables(foot_act, foot_slope, foot_count, own):
    slot = jnp.arange(K_MAX)
    same = foot_slope[:, :, None] == foot_slope[:, None, :]
    first = jnp.min(jnp.where(same, slot[None, None, :], K_MAX), axis=2)
    fresh = first == slot[None, :]
    rank = jnp.sum(fresh[:, None, :] & (slot[None, None, :] < first[:, :, None]), axis=2)
    at_rank = fresh[:, None, :] & (rank[:, None, :] == jnp.arange(DIST)[None, :, None])
    dist_tab = jnp.sum(jnp.where(at_rank, foot_slope[:, None, :], 0), axis=2)
    act = lax.dynamic_index_in_dim(foot_act, own, 0, keepdims=False)
    live = slot < lax.dynamic_index_in_dim(foot_count, own, 0, keepdims=False)
    pos = act * DIST + lax.dynamic_index_in_dim(rank, own, 0, keepdims=False)
    holds = live[None, :] & (pos[None, :] == jnp.arange(ACT_DEV * DIST)[:, None])
    slot_of = jnp.sum(jnp.where(holds, slot[None, :], 0), axis=1)
    int_tab = jnp.concatenate([slot_of, pos]).astype(jnp.int32)
    flt_tab = jnp.concatenate([jnp.any(holds, axis=1), live]).astype(F32)
    return dist_tab.astype(jnp.int32), int_tab, flt_tab


def per_device(slopes, targets, reconstructor, foot_act, foot_slope, foot_count):
    own = lax.axis_index("samp")
    dist_tab, int_tab, flt_tab = tables(foot_act[0], foot_slope[0], foot_count[0], own)
    recon = reconstructor[0, 0]
    slopes = slopes.reshape(STEPS, LOCAL, SGB, SB).transpose(0, 2, 1, 3)
    vmem, smem, anywhere = (pl.BlockSpec(memory_space=m) for m in (pltpu.VMEM, pltpu.SMEM, pl.ANY))
    grid_set = [pltpu.VMEM((SGB, LOCAL, SB), BF16)] * 8
    pick_set = [pltpu.VMEM((8, LOCAL, WIDE), BF16)] * 8
    dma = pltpu.SemaphoreType.DMA
    fitted, resid = pl.pallas_call(
        kernel,
        out_shape=(jax.ShapeDtypeStruct(recon.shape, F32),
                   jax.ShapeDtypeStruct((ACT_DEV * SB, SAMPLES), BF16)),
        in_specs=[anywhere, vmem, anywhere, smem, smem, smem],
        out_specs=(anywhere, vmem),
        scratch_shapes=[
            grid_set, grid_set, pick_set, pick_set,
            pltpu.VMEM((8, 8, LOCAL, WIDE), BF16),
            pltpu.VMEM((8, 8, LOCAL, WIDE), BF16),
            pltpu.VMEM((STEPS, SAMPLES, WIDE), BF16),
            pltpu.VMEM((ACT_DEV * DIST, SB, SB), F32),
            pltpu.VMEM((WIDE, ACT_DEV * SB), BF16),
            pltpu.VMEM((K_MAX, SB, SB), F32),
            pltpu.VMEM((K_MAX, SB, SB), F32),
            pltpu.VMEM((STEPS, 4, SAMPLES, ACT_DEV * SB), BF16),
            pltpu.VMEM((STEPS, SAMPLES, ACT_DEV * SB), F32),
            pltpu.VMEM((SAMPLES, SAMPLES), BF16),
            dma((3,)),
            dma((2, STEPS, 4, 2)), dma((2, STEPS, 4, 2)),
            dma((STEPS, 8, 8)), dma((STEPS, 8, 8)),
            dma((STEPS, 3)), dma((STEPS, 3)),
            dma((4,)),
        ],
        compiler_params=pltpu.CompilerParams(
            collective_id=0, has_side_effects=True, vmem_limit_bytes=60 * 1024 * 1024),
    )(slopes, targets, recon, dist_tab, int_tab, flt_tab)
    return fitted[None, None], resid


def solution(mesh):
    return jax.shard_map(
        per_device,
        mesh=mesh,
        in_specs=(
            P(None, "samp", "sens"),
            P(None, "samp", None),
            P("sens", "samp", None, None, None),
            P("sens", None, None),
            P("sens", None, None),
            P("sens", None),
        ),
        out_specs=(P("sens", "samp", None, None, None), P("samp", None)),
        check_vma=False,
    )
```

time: 261 us -> 100 us (0.38)
  waiting for transfers between devices: 138 us -> 0 us
  Pallas kernels: 0 us -> 87.2 us
  local copies, waits for them, and re-layouts: 53.4 us -> 5.76 us
  starting transfers between devices: 20.5 us -> 0 us
  matrix products: 19.1 us -> 0 us
  between operations: 14.2 us -> 0.69 us
  other arithmetic: 13.2 us -> 5.82 us
    pallas_call x0 -> x1, Pallas kernels: none -> 87.2 us  [per_device(): pl.pallas_call(kernel, out_shape=(jax.ShapeDtypeStruct(recon.shape, F32),...]
    all_to_all x2 -> x0, waiting for transfers between devices: 78.8 us -> none  [per_device(): lax.all_to_all(outgoing, 'samp', split_axis=1, concat_axis=0, tiled=True)]
    psum x2 -> x0, waiting for transfers between devices: 59.5 us -> none  [per_device(): total = lax.psum(summed, 'sens')]
    gather x4 -> x0, local copies, waits for them, and re-layouts: 33.1 us -> none  [the longest x2 29.1 us: per_device(): outgoing = jnp.take(local_rows, slope_all.reshape(-1), axis=1)]
    all_to_all x2 -> x0, starting transfers between devices: 20.2 us -> none  [per_device(): lax.all_to_all(outgoing, 'samp', split_axis=1, concat_axis=0, tiled=True)]
    dot_general x6 -> x0, matrix products: 19.1 us -> none  [the longest x2 8.22 us: per_device(): jnp.einsum('kin,nkl->kil', slot_residual, slot_slopes, preferred_element_...]
    select_n x2 -> x0, other arithmetic: 10.6 us -> none  [the longest x1 10.6 us: per_device(): outgoing = jnp.take(local_rows, slope_all.reshape(-1), axis=1)]
    dot_general x3 -> x0, local copies, waits for them, and re-layouts: 6.91 us -> none  [the longest x1 5.48 us: per_device(): jnp.einsum('kil,nkl->kin', weights_low, slot_slopes, preferred_element_ty...]
  transfers between devices with their start and end apart: 4 -> 0, of which waited for: 4 -> 0; matrix products, arithmetic and copies ran while one was open for 8% -> 0% of each run, Pallas kernels for 0% -> 0%
where the time goes in v1:
time: 100 us; the launch traced here: 99.5 us
  Pallas kernels  87.2 us (87%)
  other arithmetic  5.82 us (6%)
  local copies, waits for them, and re-layouts  5.76 us (6%)
    pallas_call x1, Pallas kernels, per_device(): pl.pallas_call(kernel, out_shape=(jax.ShapeDtypeStruct(recon.shape, F32),...  87.2 us
    unnamed x6, local copies, waits for them, and re-layouts  4.48 us

profile of v1, /device:TPU:1, one launch (start us, length us, event | category | flops | bytes accessed | tf_op | source)
XLA Modules:
  0.0 99.5 jit_solution(16057105185681555160)
XLA Ops:
  0.6 0.0 copy-start
  0.6 0.6 copy-done
  1.3 0.6 constant_dynamic-slice_fusion
  1.9 0.6 iota_compare_fusion.4
  2.5 0.9 fusion.5
  3.4 0.9 select_reduce_fusion
  4.4 0.1 convert_reduce_fusion
  4.5 0.9 fusion.2
  5.5 0.8 select_reduce_fusion.1
  6.3 0.1 fusion.4
  6.4 0.1 select_reduce_fusion.2
  6.5 0.7 add_convert_fusion.flt_tab
  7.1 0.6 pad_add_fusion.int_tab
  7.7 0.7 copy.17.dist_tab
  8.4 87.2 %shard_map.77 = (f32[32,128,128]{2,1,0:T(8,128)}, bf16[256,256]{1,0:T(8,128)(2,1)}) custom-call(bf16[2,294,4,128]{3,2,1,0:T(4,128)(2,1)} %bitcast.13, bf16[2,256,256]{2,1,0:T(8,128)(2,1)} %targets.1, f32[32,128,128]{2,1,0:T(8,128)} %bitcast.11, s32[64,20]{1,0:T(8,128)} %copy.17.dist_tab, s32[72]{0:T(128)} %pad_add_fusion.int_tab, f32[72]{0:T(128)} %add_convert_fusion.flt_tab), custom_call_target="tpu_custom_call" | custom-call | tf_op jit(solution)/shard_map/pallas_call | solution.py:319
  95.6 0.0 copy-start.1
  95.6 3.2 %copy.20 = f32[1,1,32,128,128]{4,3,2,1,0:T(8,128)} copy(f32[1,1,32,128,128]{4,3,2,1,0:T(8,128)} %bitcast.12) | data formatting | bytes 4194304
  98.8 0.0 copy-done.1
  98.8 0.7 copy.21
  (2 shorter events, 0.0 us)
Async XLA Ops:
  0.6 0.7 copy-start
  95.6 3.2 %copy-start.1 = (bf16[256,256]{1,0:T(8,128)(2,1)S(1)}, bf16[256,256]{1,0:T(8,128)(2,1)}, u32[]{:S(2)}) copy-start(bf16[256,256]{1,0:T(8,128)(2,1)} %get-tuple-element.11) | copy-start | bytes 393220

commit v2 on v1

--- a/solution.py
+++ b/solution.py
@@ -28,9 +28,47 @@
     return OFFS.index(4 if off == -4 else off)
 
 
-def kernel(slopes, targets, recon, dist_tab, int_tab, flt_tab, fitted, resid_out,
-           grid0, grid1, pick0, pick1, got0, got1, mat, weights, low_t, recon_v, outbuf,
-           preds, goal, perm, load_sem, zs, zr, xs, xr, ys, yr, out_sem):
+CHUNKS = ((0, 160), (160, 224), (224, 256))
+ROW_POS = 24
+ROW_SLOT = ROW_POS + K_MAX
+ROW_MASK = ROW_SLOT + ACT_DEV * DIST
+ROW_LIVE = ROW_MASK + ACT_DEV * DIST
+TAB_ROWS = ROW_LIVE + K_MAX
+
+
+def fill_tables(act, slope, count, tab):
+    n = slope.shape[1]
+    slot = lax.broadcasted_iota(jnp.int32, (K_MAX, n), 0)
+    blocks = slope[...]
+    first = jnp.full((K_MAX, n), K_MAX, jnp.int32)
+    for k in reversed(range(K_MAX)):
+        first = jnp.where(blocks == blocks[k:k + 1], k, first)
+    fresh = jnp.where(first == slot, 1, 0)
+    rank = jnp.zeros((K_MAX, n), jnp.int32)
+    for k in range(K_MAX):
+        rank = rank + jnp.where(first > k, fresh[k:k + 1], 0)
+    pos = act[...] * DIST + rank
+    live = jnp.where(slot < count[...], 1, 0)
+    order = lax.broadcasted_iota(jnp.int32, (ROW_POS, n), 0)
+    place_of = lax.broadcasted_iota(jnp.int32, (ACT_DEV * DIST, n), 0)
+    held = jnp.zeros((ROW_POS, n), jnp.int32)
+    slot_of = jnp.zeros((ACT_DEV * DIST, n), jnp.int32)
+    mask = jnp.zeros((ACT_DEV * DIST, n), jnp.int32)
+    for k in range(K_MAX):
+        held = held + jnp.where(order == rank[k:k + 1], blocks[k:k + 1] * fresh[k:k + 1], 0)
+        hit = jnp.where(place_of == pos[k:k + 1], live[k:k + 1], 0)
+        slot_of = slot_of + hit * k
+        mask = mask + hit
+    tab[0:ROW_POS, :] = held
+    tab[ROW_POS:ROW_SLOT, :] = pos
+    tab[ROW_SLOT:ROW_MASK, :] = slot_of
+    tab[ROW_MASK:ROW_LIVE, :] = mask
+    tab[ROW_LIVE:TAB_ROWS, :] = live
+
+
+def kernel(slopes, targets, recon, act, slope, count, fitted, resid_out,
+           tab_v, tab, grid0, grid1, pick0, pick1, got0, got1, mat, weights, low_t, recon_v, outbuf,
+           preds, goal, perm, resid, load_sem, zs, zr, xs, xr, ys, yr, out_sem):
     grids, picks, gots = (grid0, grid1), (pick0, pick1), (got0, got1)
     sens = lax.axis_index("sens")
     samp = lax.axis_index("samp")
@@ -77,23 +115,25 @@
             device_id_type=MESH,
         )
 
-    def y_copy(t, e):
+    def y_copy(t, c, e):
+        rows = pl.ds(CHUNKS[c][0], CHUNKS[c][1] - CHUNKS[c][0])
         return pltpu.make_async_remote_copy(
-            src_ref=preds.at[t, sens],
-            dst_ref=preds.at[t, sens],
-            send_sem=ys.at[t, e - 1],
-            recv_sem=yr.at[t, e - 1],
+            src_ref=preds.at[t, sens, rows],
+            dst_ref=preds.at[t, sens, rows],
+            send_sem=ys.at[t, c, e - 1],
+            recv_sem=yr.at[t, c, e - 1],
             device_id=((sens + e) % 4, samp),
             device_id_type=MESH,
         )
 
-    def y_arrival(t, e):
+    def y_arrival(t, c, e):
         other = (sens - e + 4) % 4
+        rows = pl.ds(CHUNKS[c][0], CHUNKS[c][1] - CHUNKS[c][0])
         return pltpu.make_async_remote_copy(
-            src_ref=preds.at[t, other],
-            dst_ref=preds.at[t, other],
-            send_sem=ys.at[t, e - 1],
-            recv_sem=yr.at[t, e - 1],
+            src_ref=preds.at[t, other, rows],
+            dst_ref=preds.at[t, other, rows],
+            send_sem=ys.at[t, c, e - 1],
+            recv_sem=yr.at[t, c, e - 1],
             device_id=(other, samp),
             device_id_type=MESH,
         )
@@ -110,7 +150,7 @@
         def one(e, to):
             row = plane * 8 + q_of(e, 1)
             for d in range(DIST):
-                to[:, d * SB:(d + 1) * SB] = src[dist_tab[row, d]]
+                to[:, d * SB:(d + 1) * SB] = src[tab[d, row]]
 
         one(0, gots[t].at[r, own_q])
 
@@ -136,25 +176,33 @@
                 block = weights[j * DIST + d].astype(BF16)
                 low_t[pl.ds(pl.multiple_of(d * SB, SB), SB), j * SB:(j + 1) * SB] = block.T
 
-    def predict(t):
-        part = jnp.dot(mat[t], low_t[...], preferred_element_type=F32)
-        preds[t, sens] = part.astype(BF16)
-
-    def residual(t):
-        total = preds[t, 0].astype(F32)
+    def predict(t, c):
+        rows = slice(*CHUNKS[c])
+        part = jnp.dot(mat[t, rows], low_t[...], preferred_element_type=F32)
+        preds[t, sens, rows] = part.astype(BF16)
+        for e in range(1, 4):
+            y_copy(t, c, e).start()
+
+    def residual(t, c):
+        rows = slice(*CHUNKS[c])
+        for e in range(1, 4):
+            y_arrival(t, c, e).wait_recv()
+        total = preds[t, 0, rows].astype(F32)
         for s in range(1, 4):
-            total = total + preds[t, s].astype(F32)
-        return (total - goal[t]).astype(BF16).T
-
-    def gradient(t, resid):
+            total = total + preds[t, s, rows].astype(F32)
+        resid[rows] = (total - goal[t, rows]).astype(BF16)
+
+    def gradient(t, lo, hi):
+        turned = resid[lo:hi].T
+
         @pl.loop(0, DIST // 2)
         def _(g):
             cols = pl.ds(pl.multiple_of(g * 2 * SB, 2 * SB), 2 * SB)
-            grad = jnp.dot(resid, mat[t, :, cols], preferred_element_type=F32)
+            grad = jnp.dot(turned, mat[t, lo:hi, cols], preferred_element_type=F32)
             for j in range(ACT_DEV):
                 for side in range(2):
                     at = j * DIST + g * 2 + side
-                    scale = RATE * flt_tab[at]
+                    scale = RATE * tab[ROW_MASK + at, samp].astype(F32)
                     weights[at] = weights[at] - scale * grad[j * SB:(j + 1) * SB, side * SB:(side + 1) * SB]
 
     own_loads = [pltpu.make_async_copy(slopes.at[t], grids[t][0], load_sem.at[t]) for t in range(STEPS)]
@@ -176,7 +224,11 @@
     for half in range(2):
         for way in range(2):
             z_copy(way, 0, 0, half).start()
+    fill_tables(act, slope, count, tab_v)
+    tab_load = pltpu.make_async_copy(tab_v, tab, load_sem.at[3])
+    tab_load.start()
     own_loads[1].wait()
+    tab_load.wait()
     pick(0, 0)
     send_picked(0, 0)
 
@@ -184,7 +236,7 @@
 
     @pl.loop(0, ACT_DEV * DIST)
     def _(at):
-        weights[at] = recon_v[int_tab[at]] * flt_tab[at]
+        weights[at] = recon_v[tab[ROW_SLOT + at, samp]] * tab[ROW_MASK + at, samp].astype(F32)
 
     low_weights()
 
@@ -217,21 +269,21 @@
         z_copy(way, 0, 3, way).wait_recv()
     pick(0, 7)
     send_picked(0, 7)
+    predict(0, 0)
     assemble(0, 5)
     assemble(0, 6)
     forward(1, 1, 0)
+    predict(0, 1)
     assemble(0, 7)
-    predict(0)
-    for e in range(1, 4):
-        y_copy(0, e).start()
+    predict(0, 2)
     forward(1, 1, 1)
     for r in (1, 2):
         pick(1, r)
         send_picked(1, r)
     assemble(1, 0)
-    for e in range(1, 4):
-        y_arrival(0, e).wait_recv()
-    gradient(0, residual(0))
+    for c in range(3):
+        residual(0, c)
+    gradient(0, 0, SAMPLES)
     forward(1, 2, 0)
     low_weights()
     forward(1, 2, 1)
@@ -247,32 +299,34 @@
         send_picked(1, r)
     assemble(1, 3)
     assemble(1, 4)
+    predict(1, 0)
     for way in range(2):
         z_copy(way, 1, 3, way).wait_recv()
     pick(1, 7)
     send_picked(1, 7)
-    for r in (5, 6, 7):
-        assemble(1, r)
-    predict(1)
-    for e in range(1, 4):
-        y_copy(1, e).start()
-    for e in range(1, 4):
-        y_arrival(1, e).wait_recv()
-    resid = residual(1)
-    gradient(1, resid)
+    assemble(1, 5)
+    assemble(1, 6)
+    predict(1, 1)
+    residual(1, 0)
+    gradient(1, *CHUNKS[0])
+    assemble(1, 7)
+    predict(1, 2)
+    residual(1, 1)
+    residual(1, 2)
+    gradient(1, CHUNKS[1][0], SAMPLES)
 
     outs = []
     for c in range(4):
         @pl.loop(c * 8, (c + 1) * 8)
         def _(k):
-            fresh = weights[int_tab[ACT_DEV * DIST + k]]
-            live = flt_tab[ACT_DEV * DIST + k]
+            fresh = weights[tab[ROW_POS + k, samp]]
+            live = tab[ROW_LIVE + k, samp].astype(F32)
             outbuf[k] = fresh * live + recon_v[k] * (1.0 - live)
 
         out = pltpu.make_async_copy(outbuf.at[pl.ds(c * 8, 8)], fitted.at[pl.ds(c * 8, 8)], out_sem.at[c])
         out.start()
         outs.append(out)
-    resid_out[...] = jnp.dot(resid, perm[...], preferred_element_type=F32).astype(BF16)
+    resid_out[...] = jnp.dot(resid[...].T, perm[...], preferred_element_type=F32).astype(BF16)
 
     for t in range(STEPS):
         for hop in range(4):
@@ -283,46 +337,30 @@
         for r in range(8):
             for e in range(1, 8):
                 x_copy(t, r, e).wait_send()
-        for e in range(1, 4):
-            y_copy(t, e).wait_send()
+        for c in range(3):
+            for e in range(1, 4):
+                y_copy(t, c, e).wait_send()
     for out in outs:
         out.wait()
 
 
-def tables(foot_act, foot_slope, foot_count, own):
-    slot = jnp.arange(K_MAX)
-    same = foot_slope[:, :, None] == foot_slope[:, None, :]
-    first = jnp.min(jnp.where(same, slot[None, None, :], K_MAX), axis=2)
-    fresh = first == slot[None, :]
-    rank = jnp.sum(fresh[:, None, :] & (slot[None, None, :] < first[:, :, None]), axis=2)
-    at_rank = fresh[:, None, :] & (rank[:, None, :] == jnp.arange(DIST)[None, :, None])
-    dist_tab = jnp.sum(jnp.where(at_rank, foot_slope[:, None, :], 0), axis=2)
-    act = lax.dynamic_index_in_dim(foot_act, own, 0, keepdims=False)
-    live = slot < lax.dynamic_index_in_dim(foot_count, own, 0, keepdims=False)
-    pos = act * DIST + lax.dynamic_index_in_dim(rank, own, 0, keepdims=False)
-    holds = live[None, :] & (pos[None, :] == jnp.arange(ACT_DEV * DIST)[:, None])
-    slot_of = jnp.sum(jnp.where(holds, slot[None, :], 0), axis=1)
-    int_tab = jnp.concatenate([slot_of, pos]).astype(jnp.int32)
-    flt_tab = jnp.concatenate([jnp.any(holds, axis=1), live]).astype(F32)
-    return dist_tab.astype(jnp.int32), int_tab, flt_tab
-
-
 def per_device(slopes, targets, reconstructor, foot_act, foot_slope, foot_count):
-    own = lax.axis_index("samp")
-    dist_tab, int_tab, flt_tab = tables(foot_act[0], foot_slope[0], foot_count[0], own)
     recon = reconstructor[0, 0]
     slopes = slopes.reshape(STEPS, LOCAL, SGB, SB).transpose(0, 2, 1, 3)
-    vmem, smem, anywhere = (pl.BlockSpec(memory_space=m) for m in (pltpu.VMEM, pltpu.SMEM, pl.ANY))
+    vmem, anywhere = (pl.BlockSpec(memory_space=m) for m in (pltpu.VMEM, pl.ANY))
     grid_set = [pltpu.VMEM((SGB, LOCAL, SB), BF16)] * 8
     pick_set = [pltpu.VMEM((8, LOCAL, WIDE), BF16)] * 8
     dma = pltpu.SemaphoreType.DMA
+    n_samp = foot_count.shape[1]
     fitted, resid = pl.pallas_call(
         kernel,
         out_shape=(jax.ShapeDtypeStruct(recon.shape, F32),
                    jax.ShapeDtypeStruct((ACT_DEV * SB, SAMPLES), BF16)),
-        in_specs=[anywhere, vmem, anywhere, smem, smem, smem],
+        in_specs=[anywhere, vmem, anywhere, vmem, vmem, vmem],
         out_specs=(anywhere, vmem),
         scratch_shapes=[
+            pltpu.VMEM((TAB_ROWS, n_samp), jnp.int32),
+            pltpu.SMEM((TAB_ROWS, n_samp), jnp.int32),
             grid_set, grid_set, pick_set, pick_set,
             pltpu.VMEM((8, 8, LOCAL, WIDE), BF16),
             pltpu.VMEM((8, 8, LOCAL, WIDE), BF16),
@@ -334,15 +372,16 @@
             pltpu.VMEM((STEPS, 4, SAMPLES, ACT_DEV * SB), BF16),
             pltpu.VMEM((STEPS, SAMPLES, ACT_DEV * SB), F32),
             pltpu.VMEM((SAMPLES, SAMPLES), BF16),
-            dma((3,)),
+            pltpu.VMEM((SAMPLES, ACT_DEV * SB), BF16),
+            dma((4,)),
             dma((2, STEPS, 4, 2)), dma((2, STEPS, 4, 2)),
             dma((STEPS, 8, 8)), dma((STEPS, 8, 8)),
-            dma((STEPS, 3)), dma((STEPS, 3)),
+            dma((STEPS, 3, 3)), dma((STEPS, 3, 3)),
             dma((4,)),
         ],
         compiler_params=pltpu.CompilerParams(
             collective_id=0, has_side_effects=True, vmem_limit_bytes=60 * 1024 * 1024),
-    )(slopes, targets, recon, dist_tab, int_tab, flt_tab)
+    )(slopes, targets, recon, foot_act[0].T, foot_slope[0].T, foot_count)
     return fitted[None, None], resid
 
 

time: 100 us -> 82.8 us (0.83)
  Pallas kernels: 87.2 us -> 78.2 us
  other arithmetic: 5.82 us -> 0 us
  local copies, waits for them, and re-layouts: 5.76 us -> 3.83 us
    pallas_call x1, Pallas kernels: 87.2 us -> 78.2 us  [per_device(): pl.pallas_call(kernel, out_shape=(jax.ShapeDtypeStruct(recon.shape, F32),...]
    reduce_sum x3 -> x0, other arithmetic: 1.07 us -> none  [the longest x1 0.82 us: tables(): dist_tab = jnp.sum(jnp.where(at_rank, foot_slope[:, None, :], 0), axis=2)]
    unnamed x6 -> x4, local copies, waits for them, and re-layouts: 4.48 us -> 3.83 us
where the time goes in v2:
time: 82.8 us; the launch traced here: 82.7 us
  Pallas kernels  78.2 us (94%)
  local copies, waits for them, and re-layouts  3.83 us (5%)
    pallas_call x1, Pallas kernels, per_device(): pl.pallas_call(kernel, out_shape=(jax.ShapeDtypeStruct(recon.shape, F32),...  78.2 us
    unnamed x4, local copies, waits for them, and re-layouts  3.83 us

profile of v2, /device:TPU:1, one launch (start us, length us, event | category | flops | bytes accessed | tf_op | source)
XLA Modules:
  0.0 82.7 jit_solution(12659752641451226591)
XLA Ops:
  0.6 78.2 %shard_map.77 = (f32[32,128,128]{2,1,0:T(8,128)}, bf16[256,256]{1,0:T(8,128)(2,1)}) custom-call(bf16[2,294,4,128]{3,2,1,0:T(4,128)(2,1)} %bitcast.13, bf16[2,256,256]{2,1,0:T(8,128)(2,1)} %targets.1, f32[32,128,128]{2,1,0:T(8,128)} %bitcast.11, s32[32,64]{1,0:T(8,128)} %bitcast.14, s32[32,64]{1,0:T(8,128)} %bitcast.15, s32[1,64]{1,0:T(1,128)} %count.1), custom_call_target="tpu_custom_call" | custom-call | tf_op jit(solution)/shard_map/pallas_call | solution.py:355
  78.8 0.0 copy-start
  78.8 3.2 %copy.10 = f32[1,1,32,128,128]{4,3,2,1,0:T(8,128)} copy(f32[1,1,32,128,128]{4,3,2,1,0:T(8,128)} %bitcast.12) | data formatting | bytes 4194304
  82.0 0.0 copy-done
  82.0 0.7 copy.11
Async XLA Ops:
  78.8 3.2 %copy-start = (bf16[256,256]{1,0:T(8,128)(2,1)S(1)}, bf16[256,256]{1,0:T(8,128)(2,1)}, u32[]{:S(2)}) copy-start(bf16[256,256]{1,0:T(8,128)(2,1)} %get-tuple-element.9) | copy-start | bytes 393220

commit v3 on v2

--- a/solution.py
+++ b/solution.py
@@ -66,9 +66,19 @@
     tab[ROW_LIVE:TAB_ROWS, :] = live
 
 
-def kernel(slopes, targets, recon, act, slope, count, fitted, resid_out,
-           tab_v, tab, grid0, grid1, pick0, pick1, got0, got1, mat, weights, low_t, recon_v, outbuf,
-           preds, goal, perm, resid, load_sem, zs, zr, xs, xr, ys, yr, out_sem):
+def sample_order(plane):
+    rows = lax.broadcasted_iota(jnp.int32, (SAMPLES, SAMPLES), 0)
+    cols = lax.broadcasted_iota(jnp.int32, (SAMPLES, SAMPLES), 1)
+    off = jnp.zeros_like(rows)
+    for r in range(8):
+        off = jnp.where(rows // 32 == r, (plane + OFFS[r] + 8) % 8, off)
+    return jnp.where(cols == off * 32 + rows % 32, 1.0, 0.0).astype(BF16)
+
+
+def kernel(slopes, targets, recon, act, slope, count, base_out, tail_out, resid, tab_out,
+           tab_v, tab, grid0, grid1, pick0, pick1, far_out, far_in, last_out, last_mid, last_in,
+           got0, got1, mat, weights, low_t, recon_v, base,
+           preds, goal, perm, load_sem, zs, zr, xs, xr, ys, yr, out_sem):
     grids, picks, gots = (grid0, grid1), (pick0, pick1), (got0, got1)
     sens = lax.axis_index("sens")
     samp = lax.axis_index("samp")
@@ -95,9 +105,35 @@
             device_id_type=MESH,
         )
 
+    def far_copy(way, t, half):
+        rows = pl.ds(half * 4, 4)
+        return pltpu.make_async_remote_copy(
+            src_ref=far_out[t][way].at[rows],
+            dst_ref=far_in[t][way].at[rows],
+            send_sem=zs.at[way, t, 2, half],
+            recv_sem=zr.at[way, t, 2, half],
+            device_id=z_dev(1 - 2 * way),
+            device_id_type=MESH,
+        )
+
+    def last_copy(way, t, hop):
+        return pltpu.make_async_remote_copy(
+            src_ref=(last_out if hop == 0 else last_mid)[t][way],
+            dst_ref=last_mid[t][way] if hop == 0 else last_in[t].at[pl.ds(way * 4, 4)],
+            send_sem=zs.at[way, t, 3, hop],
+            recv_sem=zr.at[way, t, 3, hop],
+            device_id=z_dev(1 - 2 * way),
+            device_id_type=MESH,
+        )
+
+    def x_source(t, r, e):
+        if r < 5:
+            return picks[t][r].at[e]
+        return (last_in[t] if r == 7 else far_in[t][r - 5]).at[q_of(e, 1)]
+
     def x_copy(t, r, e):
         return pltpu.make_async_remote_copy(
-            src_ref=picks[t][r].at[e],
+            src_ref=x_source(t, r, e),
             dst_ref=gots[t].at[r, own_q],
             send_sem=xs.at[t, r, e],
             recv_sem=xr.at[t, r, e],
@@ -107,7 +143,7 @@
 
     def x_arrival(t, r, e):
         return pltpu.make_async_remote_copy(
-            src_ref=picks[t][r].at[e],
+            src_ref=x_source(t, r, e),
             dst_ref=gots[t].at[r, q_of(e, -1)],
             send_sem=xs.at[t, r, e],
             recv_sem=xr.at[t, r, e],
@@ -138,29 +174,66 @@
             device_id_type=MESH,
         )
 
-    def forward(t, hop, half):
-        for way in range(2):
-            z_copy(way, t, hop - 1, half).wait_recv()
-            if hop < 3 or half == way:
-                z_copy(way, t, hop, half).start()
+    def forward(t, half):
+        for way in range(2):
+            z_copy(way, t, 0, half).wait_recv()
+            z_copy(way, t, 1, half).start()
+
+    def pick_one(src, row, to):
+        for d in range(DIST):
+            to[:, d * SB:(d + 1) * SB] = src[tab[d, row]]
 
     def pick(t, r):
-        src = grids[t][r]
-
-        def one(e, to):
-            row = plane * 8 + q_of(e, 1)
-            for d in range(DIST):
-                to[:, d * SB:(d + 1) * SB] = src[tab[d, row]]
-
-        one(0, gots[t].at[r, own_q])
+        pick_one(grids[t][r], samp, gots[t].at[r, own_q])
 
         @pl.loop(1, 8)
         def _(e):
-            one(e, picks[t][r].at[e])
-
-    def send_picked(t, r):
+            pick_one(grids[t][r], plane * 8 + q_of(e, 1), picks[t][r].at[e])
+
         for e in range(1, 8):
             x_copy(t, r, e).start()
+
+    def pick_far(t):
+        for half in range(2):
+            for way in range(2):
+                z_copy(way, t, 1, half).wait_recv()
+        for way in range(2):
+            ahead = (plane + 2 - 4 * way + 8) % 8 * 8 + way * 4
+
+            @pl.loop(0, 4)
+            def _(q):
+                pick_one(grids[t][3 + way], ahead + q, last_out[t][way].at[q])
+
+            last_copy(way, t, 0).start()
+        for half in range(2):
+            for way in range(2):
+                ahead = (plane + 1 - 2 * way + 8) % 8 * 8
+
+                @pl.loop(half * 4, half * 4 + 4)
+                def _(q):
+                    pick_one(grids[t][3 + way], ahead + q, far_out[t][way].at[q])
+
+                far_copy(way, t, half).start()
+
+    def pass_last(t):
+        for way in range(2):
+            last_copy(way, t, 0).wait_recv()
+            last_copy(way, t, 1).start()
+
+    def relay_far(t):
+        for way in range(2):
+            for half in range(2):
+                far_copy(way, t, half).wait_recv()
+            for e in range(1, 8):
+                x_copy(t, 5 + way, e).start()
+            gots[t][5 + way, own_q] = far_in[t][way][own_q]
+
+    def relay_last(t):
+        for way in range(2):
+            last_copy(way, t, 1).wait_recv()
+        for e in range(1, 8):
+            x_copy(t, 7, e).start()
+        gots[t][7, own_q] = last_in[t][own_q]
 
     def assemble(t, r):
         for e in range(1, 8):
@@ -227,10 +300,11 @@
     fill_tables(act, slope, count, tab_v)
     tab_load = pltpu.make_async_copy(tab_v, tab, load_sem.at[3])
     tab_load.start()
+    tab_keep = pltpu.make_async_copy(tab_v, tab_out, load_sem.at[4])
+    tab_keep.start()
     own_loads[1].wait()
     tab_load.wait()
     pick(0, 0)
-    send_picked(0, 0)
 
     recon_load.wait()
 
@@ -239,101 +313,84 @@
         weights[at] = recon_v[tab[ROW_SLOT + at, samp]] * tab[ROW_MASK + at, samp].astype(F32)
 
     low_weights()
-
-    rows = lax.broadcasted_iota(jnp.int32, (SAMPLES, SAMPLES), 0)
-    cols = lax.broadcasted_iota(jnp.int32, (SAMPLES, SAMPLES), 1)
-    off = jnp.zeros_like(rows)
-    for r in range(8):
-        off = jnp.where(rows // 32 == r, (plane + OFFS[r] + 8) % 8, off)
-    perm[...] = jnp.where(cols == off * 32 + rows % 32, 1.0, 0.0).astype(BF16)
+    perm[...] = sample_order(plane)
     for t in range(STEPS):
         goal[t] = lax.dot_general(perm[...], targets[t], (((1,), (1,)), ((), ())),
                                   preferred_element_type=F32)
 
-    for hop in range(1, 4):
-        for half in range(2):
-            forward(0, hop, half)
-        if hop == 3:
-            for half in range(2):
-                for way in range(2):
-                    z_copy(way, 1, 0, half).start()
-        for sign in (-1, 1):
-            pick(0, place(sign * hop))
-            send_picked(0, place(sign * hop))
-        if hop > 1:
-            for r in ((0, 1, 2) if hop == 2 else (3, 4)):
-                assemble(0, r)
+    forward(0, 0)
+    forward(0, 1)
+    for way in range(2):
+        z_copy(way, 1, 0, 0).start()
+    pick(0, 1)
+    pick(0, 2)
+    assemble(0, 0)
+    pick_far(0)
+    pick(0, 3)
+    pick(0, 4)
+    pass_last(0)
+    for way in range(2):
+        z_copy(way, 1, 0, 1).start()
+    forward(1, 0)
     pick(1, 0)
-    send_picked(1, 0)
-    for way in range(2):
-        z_copy(way, 0, 3, way).wait_recv()
-    pick(0, 7)
-    send_picked(0, 7)
+    for r in range(1, 5):
+        assemble(0, r)
     predict(0, 0)
-    assemble(0, 5)
-    assemble(0, 6)
-    forward(1, 1, 0)
+    relay_far(0)
+    relay_last(0)
+    for r in (5, 6):
+        assemble(0, r)
     predict(0, 1)
+    forward(1, 1)
     assemble(0, 7)
     predict(0, 2)
-    forward(1, 1, 1)
-    for r in (1, 2):
-        pick(1, r)
-        send_picked(1, r)
-    assemble(1, 0)
+    pick(1, 1)
+    pick(1, 2)
     for c in range(3):
         residual(0, c)
     gradient(0, 0, SAMPLES)
-    forward(1, 2, 0)
     low_weights()
-    forward(1, 2, 1)
-    for r in (3, 4):
-        pick(1, r)
-        send_picked(1, r)
+    assemble(1, 0)
+    pick_far(1)
+    pick(1, 3)
+    pick(1, 4)
+    pass_last(1)
     assemble(1, 1)
     assemble(1, 2)
-    for half in range(2):
-        forward(1, 3, half)
-    for r in (5, 6):
-        pick(1, r)
-        send_picked(1, r)
+    relay_far(1)
     assemble(1, 3)
     assemble(1, 4)
     predict(1, 0)
-    for way in range(2):
-        z_copy(way, 1, 3, way).wait_recv()
-    pick(1, 7)
-    send_picked(1, 7)
+    relay_last(1)
+    residual(1, 0)
+    gradient(1, *CHUNKS[0])
+    tail = CHUNKS[1][0]
+
+    @pl.loop(0, K_MAX)
+    def _(k):
+        live = tab[ROW_LIVE + k, samp].astype(F32)
+        base[k] = weights[tab[ROW_POS + k, samp]] * live + recon_v[k] * (1.0 - live)
+
+    outs = [pltpu.make_async_copy(base, base_out, out_sem.at[0])]
+    outs[0].start()
     assemble(1, 5)
     assemble(1, 6)
     predict(1, 1)
-    residual(1, 0)
-    gradient(1, *CHUNKS[0])
     assemble(1, 7)
     predict(1, 2)
+    outs.append(pltpu.make_async_copy(mat.at[1, pl.ds(tail, SAMPLES - tail)], tail_out, out_sem.at[1]))
+    outs[1].start()
     residual(1, 1)
     residual(1, 2)
-    gradient(1, CHUNKS[1][0], SAMPLES)
-
-    outs = []
-    for c in range(4):
-        @pl.loop(c * 8, (c + 1) * 8)
-        def _(k):
-            fresh = weights[tab[ROW_POS + k, samp]]
-            live = tab[ROW_LIVE + k, samp].astype(F32)
-            outbuf[k] = fresh * live + recon_v[k] * (1.0 - live)
-
-        out = pltpu.make_async_copy(outbuf.at[pl.ds(c * 8, 8)], fitted.at[pl.ds(c * 8, 8)], out_sem.at[c])
-        out.start()
-        outs.append(out)
-    resid_out[...] = jnp.dot(resid[...].T, perm[...], preferred_element_type=F32).astype(BF16)
+    outs.append(tab_keep)
 
     for t in range(STEPS):
-        for hop in range(4):
+        for way in range(2):
             for half in range(2):
-                for way in range(2):
-                    if hop < 3 or half == way:
-                        z_copy(way, t, hop, half).wait_send()
+                for hop in range(2):
+                    z_copy(way, t, hop, half).wait_send()
+                far_copy(way, t, half).wait_send()
+                last_copy(way, t, half).wait_send()
         for r in range(8):
             for e in range(1, 8):
                 x_copy(t, r, e).wait_send()
@@ -344,24 +401,63 @@
         out.wait()
 
 
+def finish(base_in, recent, resid, tab, fitted, resid_out, base, fresh, load_sem, out_sem):
+    samp = lax.axis_index("samp")
+    tail = CHUNKS[1][0]
+    each = K_MAX // 4
+
+    def load(c):
+        rows = pl.ds(c * each, each)
+        return pltpu.make_async_copy(base_in.at[rows], base.at[rows], load_sem.at[c])
+
+    def store(c):
+        rows = pl.ds(c * each, each)
+        return pltpu.make_async_copy(fresh.at[rows], fitted.at[rows], out_sem.at[c])
+
+    for c in range(4):
+        load(c).start()
+    turned = resid[...].T
+    resid_out[...] = jnp.dot(turned, sample_order(samp // 8), preferred_element_type=F32).astype(BF16)
+    for c in range(4):
+        load(c).wait()
+        for k in range(c * each, (c + 1) * each):
+            pos = tab[ROW_POS + k, samp]
+            scale = RATE * tab[ROW_LIVE + k, samp].astype(F32)
+            act = pos // DIST
+            lanes = pl.ds(pl.multiple_of(act * SB, SB), SB)
+            cols = pl.ds(pl.multiple_of((pos - act * DIST) * SB, SB), SB)
+            grad = lax.dot_general(resid[tail:, lanes], recent[:, cols], (((0,), (0,)), ((), ())),
+                                   preferred_element_type=F32)
+            fresh[k] = base[k] - scale * grad
+        store(c).start()
+    for c in range(4):
+        store(c).wait()
+
+
 def per_device(slopes, targets, reconstructor, foot_act, foot_slope, foot_count):
     recon = reconstructor[0, 0]
     slopes = slopes.reshape(STEPS, LOCAL, SGB, SB).transpose(0, 2, 1, 3)
-    vmem, anywhere = (pl.BlockSpec(memory_space=m) for m in (pltpu.VMEM, pl.ANY))
-    grid_set = [pltpu.VMEM((SGB, LOCAL, SB), BF16)] * 8
-    pick_set = [pltpu.VMEM((8, LOCAL, WIDE), BF16)] * 8
+    vmem, smem, anywhere = (pl.BlockSpec(memory_space=m) for m in (pltpu.VMEM, pltpu.SMEM, pl.ANY))
+    grid_set = [pltpu.VMEM((SGB, LOCAL, SB), BF16)] * 5
+    pick_set = [pltpu.VMEM((8, LOCAL, WIDE), BF16)] * 5
+    far_set = [[pltpu.VMEM((8, LOCAL, WIDE), BF16)] * 2] * STEPS
+    last_set = [[pltpu.VMEM((4, LOCAL, WIDE), BF16)] * 2] * STEPS
     dma = pltpu.SemaphoreType.DMA
     n_samp = foot_count.shape[1]
-    fitted, resid = pl.pallas_call(
+    tail = SAMPLES - CHUNKS[1][0]
+    base, recent, resid, tab = pl.pallas_call(
         kernel,
         out_shape=(jax.ShapeDtypeStruct(recon.shape, F32),
-                   jax.ShapeDtypeStruct((ACT_DEV * SB, SAMPLES), BF16)),
+                   jax.ShapeDtypeStruct((tail, WIDE), BF16),
+                   jax.ShapeDtypeStruct((SAMPLES, ACT_DEV * SB), BF16),
+                   jax.ShapeDtypeStruct((TAB_ROWS, n_samp), jnp.int32)),
         in_specs=[anywhere, vmem, anywhere, vmem, vmem, vmem],
-        out_specs=(anywhere, vmem),
+        out_specs=(anywhere, anywhere, vmem, anywhere),
         scratch_shapes=[
             pltpu.VMEM((TAB_ROWS, n_samp), jnp.int32),
             pltpu.SMEM((TAB_ROWS, n_samp), jnp.int32),
             grid_set, grid_set, pick_set, pick_set,
+            far_set, far_set, last_set, last_set, [pltpu.VMEM((8, LOCAL, WIDE), BF16)] * STEPS,
             pltpu.VMEM((8, 8, LOCAL, WIDE), BF16),
             pltpu.VMEM((8, 8, LOCAL, WIDE), BF16),
             pltpu.VMEM((STEPS, SAMPLES, WIDE), BF16),
@@ -372,17 +468,26 @@
             pltpu.VMEM((STEPS, 4, SAMPLES, ACT_DEV * SB), BF16),
             pltpu.VMEM((STEPS, SAMPLES, ACT_DEV * SB), F32),
             pltpu.VMEM((SAMPLES, SAMPLES), BF16),
-            pltpu.VMEM((SAMPLES, ACT_DEV * SB), BF16),
-            dma((4,)),
+            dma((5,)),
             dma((2, STEPS, 4, 2)), dma((2, STEPS, 4, 2)),
             dma((STEPS, 8, 8)), dma((STEPS, 8, 8)),
             dma((STEPS, 3, 3)), dma((STEPS, 3, 3)),
-            dma((4,)),
+            dma((2,)),
         ],
         compiler_params=pltpu.CompilerParams(
-            collective_id=0, has_side_effects=True, vmem_limit_bytes=60 * 1024 * 1024),
+            collective_id=0, has_side_effects=True, vmem_limit_bytes=40 * 1024 * 1024),
     )(slopes, targets, recon, foot_act[0].T, foot_slope[0].T, foot_count)
-    return fitted[None, None], resid
+    fitted, fit_residual = pl.pallas_call(
+        finish,
+        out_shape=(jax.ShapeDtypeStruct(recon.shape, F32),
+                   jax.ShapeDtypeStruct((ACT_DEV * SB, SAMPLES), BF16)),
+        in_specs=[anywhere, vmem, vmem, smem],
+        out_specs=(anywhere, vmem),
+        scratch_shapes=[pltpu.VMEM(recon.shape, F32), pltpu.VMEM(recon.shape, F32),
+                        dma((4,)), dma((4,))],
+        compiler_params=pltpu.CompilerParams(vmem_limit_bytes=16 * 1024 * 1024),
+    )(base, recent, resid, tab)
+    return fitted[None, None], fit_residual
 
 
 def solution(mesh):

time: 82.8 us -> 83.8 us (1.012)
  local copies, waits for them, and re-layouts: 3.83 us -> 5.69 us
  Pallas kernels: 78.2 us -> 77.2 us
    pallas_call x1, Pallas kernels: 78.2 us -> 72.1 us  [per_device(): pl.pallas_call(kernel, out_shape=(jax.ShapeDtypeStruct(recon.shape, F32),...]
    pallas_call x0 -> x1, Pallas kernels: none -> 5.03 us  [per_device(): pl.pallas_call(finish, out_shape=(jax.ShapeDtypeStruct(recon.shape, F32),...]
    unnamed x4 -> x12, local copies, waits for them, and re-layouts: 3.83 us -> 5.69 us
where the time goes in v3:
time: 83.8 us; the launch traced here: 83.5 us
  Pallas kernels  77.2 us (92%)
  local copies, waits for them, and re-layouts  5.69 us (7%)
    pallas_call x1, Pallas kernels, per_device(): pl.pallas_call(kernel, out_shape=(jax.ShapeDtypeStruct(recon.shape, F32),...  72.1 us
    unnamed x12, local copies, waits for them, and re-layouts  5.69 us
    pallas_call x1, Pallas kernels, per_device(): pl.pallas_call(finish, out_shape=(jax.ShapeDtypeStruct(recon.shape, F32),...  5.03 us

profile of v3, /device:TPU:1, one launch (start us, length us, event | category | flops | bytes accessed | tf_op | source)
XLA Modules:
  0.0 83.5 jit_solution(3816831157276746247)
XLA Ops:
  0.6 0.0 copy-start
  0.6 1.6 %copy-done = f32[1,1,32,128,128]{4,3,2,1,0:T(8,128)S(1)} copy-done((f32[1,1,32,128,128]{4,3,2,1,0:T(8,128)S(1)}, f32[1,1,32,128,128]{4,3,2,1,0:T(8,128)}, u32[]{:S(2)}) %copy-start) | copy-done | bytes 2097176
  2.2 0.0 copy-start.1
  2.2 1.1 %copy-done.1 = bf16[2,4,37632]{2,1,0:T(4,128)(2,1)S(1)} copy-done((bf16[2,4,37632]{2,1,0:T(4,128)(2,1)S(1)}, bf16[2,4,37632]{2,1,0:T(4,128)(2,1)}, u32[]{:S(2)}) %copy-start.1) | copy-done | bytes 602136
  3.3 0.0 copy-start.2
  3.3 0.9 %copy-done.2 = bf16[2,256,256]{2,1,0:T(8,128)(2,1)S(1)} copy-done((bf16[2,256,256]{2,1,0:T(8,128)(2,1)S(1)}, bf16[2,256,256]{2,1,0:T(8,128)(2,1)}, u32[]{:S(2)}) %copy-start.2) | copy-done | bytes 262168
  4.2 0.0 copy-start.3
  4.2 0.7 copy-done.3
  5.0 0.0 copy-start.4
  5.0 0.7 copy-done.4
  5.7 0.0 copy-start.5
  5.7 0.7 copy-done.5
  6.3 72.1 %shard_map.77 = (f32[32,128,128]{2,1,0:T(8,128)S(1)}, bf16[96,2560]{1,0:T(8,128)(2,1)S(1)}, bf16[256,256]{1,0:T(8,128)(2,1)S(1)}, s32[168,64]{1,0:T(8,128)S(1)}) custom-call(bf16[2,294,4,128]{3,2,1,0:T(4,128)(2,1)S(1)} %bitcast.12, bf16[2,256,256]{2,1,0:T(8,128)(2,1)S(1)} %copy-done.2, f32[32,128,128]{2,1,0:T(8,128)S(1)} %bitcast.11, s32[32,64]{1,0:T(8,128)S(1)} %bitcast.13, ...), custom_call_target="tpu_custom_call" | custom-call | tf_op jit(solution)/shard_map/pallas_call | solution.py:448
  78.5 5.0 %shard_map.78 = (f32[32,128,128]{2,1,0:T(8,128)}, bf16[256,256]{1,0:T(8,128)(2,1)}) custom-call(f32[32,128,128]{2,1,0:T(8,128)S(1)} %get-tuple-element.8.base_in, bf16[96,2560]{1,0:T(8,128)(2,1)S(1)} %get-tuple-element.9.recent, bf16[256,256]{1,0:T(8,128)(2,1)S(1)} %get-tuple-element.10.resid, s32[168,64]{1,0:T(8,128)S(1)} %get-tuple-element.11.tab), custom_call_target="tpu_custom_call" | custom-call | tf_op jit(solution)/shard_map/pallas_call | solution.py:480
Async XLA Ops:
  0.6 1.6 %copy-start = (f32[1,1,32,128,128]{4,3,2,1,0:T(8,128)S(1)}, f32[1,1,32,128,128]{4,3,2,1,0:T(8,128)}, u32[]{:S(2)}) copy-start(f32[1,1,32,128,128]{4,3,2,1,0:T(8,128)} %param.8) | copy-start | bytes 6291460
  2.2 1.1 %copy-start.1 = (bf16[2,4,37632]{2,1,0:T(4,128)(2,1)S(1)}, bf16[2,4,37632]{2,1,0:T(4,128)(2,1)}, u32[]{:S(2)}) copy-start(bf16[2,4,37632]{2,1,0:T(4,128)(2,1)} %param.6) | copy-start | bytes 1806340
  3.3 0.9 %copy-start.2 = (bf16[2,256,256]{2,1,0:T(8,128)(2,1)S(1)}, bf16[2,256,256]{2,1,0:T(8,128)(2,1)}, u32[]{:S(2)}) copy-start(bf16[2,256,256]{2,1,0:T(8,128)(2,1)} %targets.1) | copy-start | bytes 786436
  4.2 0.7 copy-start.3
  5.0 0.7 copy-start.4
  5.7 0.7 copy-start.5

commit v4 on v3

--- a/solution.py
+++ b/solution.py
@@ -75,8 +75,8 @@
     return jnp.where(cols == off * 32 + rows % 32, 1.0, 0.0).astype(BF16)
 
 
-def kernel(slopes, targets, recon, act, slope, count, base_out, tail_out, resid, tab_out,
-           tab_v, tab, grid0, grid1, pick0, pick1, far_out, far_in, last_out, last_mid, last_in,
+def kernel(slopes, targets_in, recon, act_in, slope_in, count_in, base_out, tail_out, resid, tab_out,
+           targets, act, slope, count, tab_v, tab, grid0, grid1, pick0, pick1, far_out, far_in, last_out, last_mid, last_in,
            got0, got1, mat, weights, low_t, recon_v, base,
            preds, goal, perm, load_sem, zs, zr, xs, xr, ys, yr, out_sem):
     grids, picks, gots = (grid0, grid1), (pick0, pick1), (got0, got1)
@@ -280,8 +280,12 @@
 
     own_loads = [pltpu.make_async_copy(slopes.at[t], grids[t][0], load_sem.at[t]) for t in range(STEPS)]
     recon_load = pltpu.make_async_copy(recon, recon_v, load_sem.at[2])
-    for load in own_loads:
+    small_loads = [pltpu.make_async_copy(src, dst, load_sem.at[5 + i]) for i, (src, dst) in enumerate(
+        ((slope_in, slope), (act_in, act), (count_in, count), (targets_in, targets)))]
+    own_loads[0].start()
+    for load in small_loads:
         load.start()
+    own_loads[1].start()
     recon_load.start()
 
     barrier = pltpu.get_barrier_semaphore()
@@ -297,6 +301,8 @@
     for half in range(2):
         for way in range(2):
             z_copy(way, 0, 0, half).start()
+    for load in small_loads:
+        load.wait()
     fill_tables(act, slope, count, tab_v)
     tab_load = pltpu.make_async_copy(tab_v, tab, load_sem.at[3])
     tab_load.start()
@@ -401,7 +407,7 @@
         out.wait()
 
 
-def finish(base_in, recent, resid, tab, fitted, resid_out, base, fresh, load_sem, out_sem):
+def finish(base_in, recent, resid, tab, fitted, resid_out, base, fresh, grad, load_sem, out_sem):
     samp = lax.axis_index("samp")
     tail = CHUNKS[1][0]
     each = K_MAX // 4
@@ -417,19 +423,22 @@
     for c in range(4):
         load(c).start()
     turned = resid[...].T
-    resid_out[...] = jnp.dot(turned, sample_order(samp // 8), preferred_element_type=F32).astype(BF16)
+    late = turned[:, tail:]
+    for g in range(DIST // 2):
+        part = jnp.dot(late, recent[:, g * 2 * SB:(g + 1) * 2 * SB], preferred_element_type=F32)
+        for j in range(ACT_DEV):
+            for side in range(2):
+                grad[j * DIST + g * 2 + side] = part[j * SB:(j + 1) * SB, side * SB:(side + 1) * SB]
     for c in range(4):
         load(c).wait()
-        for k in range(c * each, (c + 1) * each):
-            pos = tab[ROW_POS + k, samp]
+
+        @pl.loop(c * each, (c + 1) * each)
+        def _(k):
             scale = RATE * tab[ROW_LIVE + k, samp].astype(F32)
-            act = pos // DIST
-            lanes = pl.ds(pl.multiple_of(act * SB, SB), SB)
-            cols = pl.ds(pl.multiple_of((pos - act * DIST) * SB, SB), SB)
-            grad = lax.dot_general(resid[tail:, lanes], recent[:, cols], (((0,), (0,)), ((), ())),
-                                   preferred_element_type=F32)
-            fresh[k] = base[k] - scale * grad
+            fresh[k] = base[k] - scale * grad[tab[ROW_POS + k, samp]]
+
         store(c).start()
+    resid_out[...] = jnp.dot(turned, sample_order(samp // 8), preferred_element_type=F32).astype(BF16)
     for c in range(4):
         store(c).wait()
 
@@ -451,9 +460,13 @@
                    jax.ShapeDtypeStruct((tail, WIDE), BF16),
                    jax.ShapeDtypeStruct((SAMPLES, ACT_DEV * SB), BF16),
                    jax.ShapeDtypeStruct((TAB_ROWS, n_samp), jnp.int32)),
-        in_specs=[anywhere, vmem, anywhere, vmem, vmem, vmem],
+        in_specs=[pl.BlockSpec(memory_space=pltpu.HBM)] * 6,
         out_specs=(anywhere, anywhere, vmem, anywhere),
         scratch_shapes=[
+            pltpu.VMEM(targets.shape, BF16),
+            pltpu.VMEM((K_MAX, n_samp), jnp.int32),
+            pltpu.VMEM((K_MAX, n_samp), jnp.int32),
+            pltpu.VMEM((1, n_samp), jnp.int32),
             pltpu.VMEM((TAB_ROWS, n_samp), jnp.int32),
             pltpu.SMEM((TAB_ROWS, n_samp), jnp.int32),
             grid_set, grid_set, pick_set, pick_set,
@@ -468,7 +481,7 @@
             pltpu.VMEM((STEPS, 4, SAMPLES, ACT_DEV * SB), BF16),
             pltpu.VMEM((STEPS, SAMPLES, ACT_DEV * SB), F32),
             pltpu.VMEM((SAMPLES, SAMPLES), BF16),
-            dma((5,)),
+            dma((9,)),
             dma((2, STEPS, 4, 2)), dma((2, STEPS, 4, 2)),
             dma((STEPS, 8, 8)), dma((STEPS, 8, 8)),
             dma((STEPS, 3, 3)), dma((STEPS, 3, 3)),
@@ -476,7 +489,8 @@
         ],
         compiler_params=pltpu.CompilerParams(
             collective_id=0, has_side_effects=True, vmem_limit_bytes=40 * 1024 * 1024),
-    )(slopes, targets, recon, foot_act[0].T, foot_slope[0].T, foot_count)
+    )(*(pltpu.with_memory_space_constraint(x, pltpu.HBM) for x in (
+        slopes, targets, recon, foot_act[0].T, foot_slope[0].T, foot_count)))
     fitted, fit_residual = pl.pallas_call(
         finish,
         out_shape=(jax.ShapeDtypeStruct(recon.shape, F32),
@@ -484,6 +498,7 @@
         in_specs=[anywhere, vmem, vmem, smem],
         out_specs=(anywhere, vmem),
         scratch_shapes=[pltpu.VMEM(recon.shape, F32), pltpu.VMEM(recon.shape, F32),
+                        pltpu.VMEM((ACT_DEV * DIST, SB, SB), F32),
                         dma((4,)), dma((4,))],
         compiler_params=pltpu.CompilerParams(vmem_limit_bytes=16 * 1024 * 1024),
     )(base, recent, resid, tab)

time: 83.8 us -> 77.7 us (0.927)
  local copies, waits for them, and re-layouts: 5.69 us -> 0 us
    unnamed x12 -> x0, local copies, waits for them, and re-layouts: 5.69 us -> none
where the time goes in v4:
time: 77.7 us; the launch traced here: 77.6 us
  Pallas kernels  76.9 us (99%)
    pallas_call x1, Pallas kernels, per_device(): pl.pallas_call(kernel, out_shape=(jax.ShapeDtypeStruct(recon.shape, F32),...  72 us
    pallas_call x1, Pallas kernels, per_device(): pl.pallas_call(finish, out_shape=(jax.ShapeDtypeStruct(recon.shape, F32),...  4.92 us

profile of v4, /device:TPU:1, one launch (start us, length us, event | category | flops | bytes accessed | tf_op | source)
XLA Modules:
  0.0 77.6 jit_solution(11821938479391767673)
XLA Ops:
  0.6 72.0 %shard_map.77 = (f32[32,128,128]{2,1,0:T(8,128)S(1)}, bf16[96,2560]{1,0:T(8,128)(2,1)S(1)}, bf16[256,256]{1,0:T(8,128)(2,1)S(1)}, s32[168,64]{1,0:T(8,128)S(1)}) custom-call(bf16[2,294,4,128]{3,2,1,0:T(4,128)(2,1)} %bitcast.12, bf16[2,256,256]{2,1,0:T(8,128)(2,1)} %targets_in.1, f32[32,128,128]{2,1,0:T(8,128)} %bitcast.11, s32[32,64]{1,0:T(8,128)} %bitcast.13, ...), custom_call_target="tpu_custom_call" | custom-call | tf_op jit(solution)/shard_map/pallas_call | solution.py:457
  72.7 4.9 %shard_map.78 = (f32[32,128,128]{2,1,0:T(8,128)}, bf16[256,256]{1,0:T(8,128)(2,1)}) custom-call(f32[32,128,128]{2,1,0:T(8,128)S(1)} %get-tuple-element.8.base_in, bf16[96,2560]{1,0:T(8,128)(2,1)S(1)} %get-tuple-element.9.recent, bf16[256,256]{1,0:T(8,128)(2,1)S(1)} %get-tuple-element.10.resid, s32[168,64]{1,0:T(8,128)S(1)} %get-tuple-element.11.tab), custom_call_target="tpu_custom_call" | custom-call | tf_op jit(solution)/shard_map/pallas_call | solution.py:494

commit v5 on v4

--- a/solution.py
+++ b/solution.py
@@ -28,7 +28,7 @@
     return OFFS.index(4 if off == -4 else off)
 
 
-CHUNKS = ((0, 160), (160, 224), (224, 256))
+CHUNKS = ((0, 96), (96, 160), (160, 224), (224, 256))
 ROW_POS = 24
 ROW_SLOT = ROW_POS + K_MAX
 ROW_MASK = ROW_SLOT + ACT_DEV * DIST
@@ -75,10 +75,10 @@
     return jnp.where(cols == off * 32 + rows % 32, 1.0, 0.0).astype(BF16)
 
 
-def kernel(slopes, targets_in, recon, act_in, slope_in, count_in, base_out, tail_out, resid, tab_out,
-           targets, act, slope, count, tab_v, tab, grid0, grid1, pick0, pick1, far_out, far_in, last_out, last_mid, last_in,
-           got0, got1, mat, weights, low_t, recon_v, base,
-           preds, goal, perm, load_sem, zs, zr, xs, xr, ys, yr, out_sem):
+def kernel(slopes, targets_in, recon, act_in, slope_in, count_in, fresh, resid_out,
+           targets, act, slope, count, tab_v, tab, grid0, grid1, pick0, pick1, far_out, far_in, last_out, last_mid,
+           got0, got1, mat, weights, low_t, recon_v, grad_v, resid,
+           preds, goal, perm, load_sem, zs, zr, xs, xr, ys, yr):
     grids, picks, gots = (grid0, grid1), (pick0, pick1), (got0, got1)
     sens = lax.axis_index("sens")
     samp = lax.axis_index("samp")
@@ -116,20 +116,41 @@
             device_id_type=MESH,
         )
 
-    def last_copy(way, t, hop):
-        return pltpu.make_async_remote_copy(
-            src_ref=(last_out if hop == 0 else last_mid)[t][way],
-            dst_ref=last_mid[t][way] if hop == 0 else last_in[t].at[pl.ds(way * 4, 4)],
-            send_sem=zs.at[way, t, 3, hop],
-            recv_sem=zr.at[way, t, 3, hop],
+    def mid_copy(way, t):
+        return pltpu.make_async_remote_copy(
+            src_ref=last_out[t][way],
+            dst_ref=last_mid[t][way],
+            send_sem=zs.at[way, t, 3, 0],
+            recv_sem=zr.at[way, t, 3, 0],
             device_id=z_dev(1 - 2 * way),
+            device_id_type=MESH,
+        )
+
+    def last_copy(way, t, i):
+        return pltpu.make_async_remote_copy(
+            src_ref=last_mid[t][way].at[i],
+            dst_ref=gots[t].at[7, own_q],
+            send_sem=xs.at[t, 7, way * 4 + i],
+            recv_sem=xr.at[t, 7, own_q],
+            device_id=(sens, (plane + 1 - 2 * way + 8) % 8 * 8 + way * 4 + i),
+            device_id_type=MESH,
+        )
+
+    def last_arrival(t, q):
+        back = (plane - 1 + 2 * (own_q // 4) + 8) % 8
+        return pltpu.make_async_remote_copy(
+            src_ref=last_mid[t][0].at[0],
+            dst_ref=gots[t].at[7, q],
+            send_sem=xs.at[t, 7, q],
+            recv_sem=xr.at[t, 7, q],
+            device_id=(sens, back * 8 + q),
             device_id_type=MESH,
         )
 
     def x_source(t, r, e):
         if r < 5:
             return picks[t][r].at[e]
-        return (last_in[t] if r == 7 else far_in[t][r - 5]).at[q_of(e, 1)]
+        return far_in[t][r - 5].at[q_of(e, 1)]
 
     def x_copy(t, r, e):
         return pltpu.make_async_remote_copy(
@@ -204,7 +225,7 @@
             def _(q):
                 pick_one(grids[t][3 + way], ahead + q, last_out[t][way].at[q])
 
-            last_copy(way, t, 0).start()
+            mid_copy(way, t).start()
         for half in range(2):
             for way in range(2):
                 ahead = (plane + 1 - 2 * way + 8) % 8 * 8
@@ -217,27 +238,30 @@
 
     def pass_last(t):
         for way in range(2):
-            last_copy(way, t, 0).wait_recv()
-            last_copy(way, t, 1).start()
-
-    def relay_far(t):
+            mid_copy(way, t).wait_recv()
+            for i in range(4):
+                last_copy(way, t, i).start()
+
+    def relay_far(t, half):
         for way in range(2):
-            for half in range(2):
-                far_copy(way, t, half).wait_recv()
-            for e in range(1, 8):
-                x_copy(t, 5 + way, e).start()
-            gots[t][5 + way, own_q] = far_in[t][way][own_q]
-
-    def relay_last(t):
-        for way in range(2):
-            last_copy(way, t, 1).wait_recv()
-        for e in range(1, 8):
-            x_copy(t, 7, e).start()
-        gots[t][7, own_q] = last_in[t][own_q]
+            far_copy(way, t, half).wait_recv()
+            for q in range(half * 4, half * 4 + 4):
+                e = ((q // 2 - col + 4) % 4) * 2 + (q + core) % 2
+
+                @pl.when(own_q != q)
+                def _():
+                    x_copy(t, 5 + way, e).start()
+
+            @pl.when(own_q // 4 == half)
+            def _():
+                gots[t][5 + way, own_q] = far_in[t][way][own_q]
 
     def assemble(t, r):
-        for e in range(1, 8):
-            x_arrival(t, r, e).wait_recv()
+        for e in range(8):
+            if r == 7:
+                last_arrival(t, e).wait_recv()
+            elif e > 0:
+                x_arrival(t, r, e).wait_recv()
         for half in range(2):
             piece = jnp.concatenate([gots[t][r, half * 4 + q] for q in range(4)], axis=0)
             mat[t, pl.ds(r * 32 + half * 16, 16), :] = piece
@@ -276,7 +300,11 @@
                 for side in range(2):
                     at = j * DIST + g * 2 + side
                     scale = RATE * tab[ROW_MASK + at, samp].astype(F32)
-                    weights[at] = weights[at] - scale * grad[j * SB:(j + 1) * SB, side * SB:(side + 1) * SB]
+                    new = weights[at] - scale * grad[j * SB:(j + 1) * SB, side * SB:(side + 1) * SB]
+                    weights[at] = new
+                    if t == 0:
+                        lanes = pl.ds(pl.multiple_of((g * 2 + side) * SB, SB), SB)
+                        low_t[lanes, j * SB:(j + 1) * SB] = new.astype(BF16).T
 
     own_loads = [pltpu.make_async_copy(slopes.at[t], grids[t][0], load_sem.at[t]) for t in range(STEPS)]
     recon_load = pltpu.make_async_copy(recon, recon_v, load_sem.at[2])
@@ -295,7 +323,10 @@
         pl.semaphore_signal(barrier, inc=1, device_id=(sens, plane * 8 + q_of(e, 1)), device_id_type=MESH)
     for e in range(1, 4):
         pl.semaphore_signal(barrier, inc=1, device_id=((sens + e) % 4, samp), device_id_type=MESH)
-    pl.semaphore_wait(barrier, 12)
+    for q in range(8):
+        back = (plane - 1 + 2 * (own_q // 4) + 8) % 8
+        pl.semaphore_signal(barrier, inc=1, device_id=(sens, back * 8 + q), device_id_type=MESH)
+    pl.semaphore_wait(barrier, 20)
 
     own_loads[0].wait()
     for half in range(2):
@@ -306,8 +337,6 @@
     fill_tables(act, slope, count, tab_v)
     tab_load = pltpu.make_async_copy(tab_v, tab, load_sem.at[3])
     tab_load.start()
-    tab_keep = pltpu.make_async_copy(tab_v, tab_out, load_sem.at[4])
-    tab_keep.start()
     own_loads[1].wait()
     tab_load.wait()
     pick(0, 0)
@@ -334,61 +363,73 @@
     pick_far(0)
     pick(0, 3)
     pick(0, 4)
+    assemble(0, 1)
+    assemble(0, 2)
+    predict(0, 0)
     pass_last(0)
     for way in range(2):
         z_copy(way, 1, 0, 1).start()
     forward(1, 0)
     pick(1, 0)
-    for r in range(1, 5):
-        assemble(0, r)
-    predict(0, 0)
-    relay_far(0)
-    relay_last(0)
-    for r in (5, 6):
-        assemble(0, r)
+    relay_far(0, 0)
+    assemble(0, 3)
+    assemble(0, 4)
     predict(0, 1)
+    relay_far(0, 1)
+    residual(0, 0)
+    assemble(0, 5)
+    assemble(0, 6)
+    predict(0, 2)
     forward(1, 1)
     assemble(0, 7)
-    predict(0, 2)
+    predict(0, 3)
     pick(1, 1)
     pick(1, 2)
-    for c in range(3):
-        residual(0, c)
-    gradient(0, 0, SAMPLES)
-    low_weights()
-    assemble(1, 0)
     pick_far(1)
     pick(1, 3)
     pick(1, 4)
+    assemble(1, 0)
+    for c in range(1, 4):
+        residual(0, c)
+    gradient(0, 0, SAMPLES)
     pass_last(1)
     assemble(1, 1)
     assemble(1, 2)
-    relay_far(1)
+    predict(1, 0)
+    relay_far(1, 0)
+    relay_far(1, 1)
     assemble(1, 3)
     assemble(1, 4)
-    predict(1, 0)
-    relay_last(1)
-    residual(1, 0)
-    gradient(1, *CHUNKS[0])
-    tail = CHUNKS[1][0]
+    predict(1, 1)
+    assemble(1, 5)
+    assemble(1, 6)
+    predict(1, 2)
+    assemble(1, 7)
+    predict(1, 3)
+    tail = CHUNKS[3][0]
+    for c in range(3):
+        residual(1, c)
+    gradient(1, 0, tail)
 
     @pl.loop(0, K_MAX)
     def _(k):
         live = tab[ROW_LIVE + k, samp].astype(F32)
-        base[k] = weights[tab[ROW_POS + k, samp]] * live + recon_v[k] * (1.0 - live)
-
-    outs = [pltpu.make_async_copy(base, base_out, out_sem.at[0])]
-    outs[0].start()
-    assemble(1, 5)
-    assemble(1, 6)
-    predict(1, 1)
-    assemble(1, 7)
-    predict(1, 2)
-    outs.append(pltpu.make_async_copy(mat.at[1, pl.ds(tail, SAMPLES - tail)], tail_out, out_sem.at[1]))
-    outs[1].start()
-    residual(1, 1)
-    residual(1, 2)
-    outs.append(tab_keep)
+        fresh[k] = weights[tab[ROW_POS + k, samp]] * live + recon_v[k] * (1.0 - live)
+
+    residual(1, 3)
+    turned = resid[...].T
+    late = turned[:, tail:]
+    for g in range(DIST // 2):
+        part = jnp.dot(late, mat[1, tail:, g * 2 * SB:(g + 1) * 2 * SB], preferred_element_type=F32)
+        for j in range(ACT_DEV):
+            for side in range(2):
+                grad_v[j * DIST + g * 2 + side] = part[j * SB:(j + 1) * SB, side * SB:(side + 1) * SB]
+    resid_out[...] = jnp.dot(turned, perm[...], preferred_element_type=F32).astype(BF16)
+
+    @pl.loop(0, K_MAX)
+    def _(k):
+        scale = RATE * tab[ROW_LIVE + k, samp].astype(F32)
+        fresh[k] = fresh[k] - scale * grad_v[tab[ROW_POS + k, samp]]
 
     for t in range(STEPS):
         for way in range(2):
@@ -396,72 +437,33 @@
                 for hop in range(2):
                     z_copy(way, t, hop, half).wait_send()
                 far_copy(way, t, half).wait_send()
-                last_copy(way, t, half).wait_send()
-        for r in range(8):
+            mid_copy(way, t).wait_send()
+            for i in range(4):
+                last_copy(way, t, i).wait_send()
+        for r in range(7):
             for e in range(1, 8):
                 x_copy(t, r, e).wait_send()
-        for c in range(3):
+        for c in range(len(CHUNKS)):
             for e in range(1, 4):
                 y_copy(t, c, e).wait_send()
-    for out in outs:
-        out.wait()
-
-
-def finish(base_in, recent, resid, tab, fitted, resid_out, base, fresh, grad, load_sem, out_sem):
-    samp = lax.axis_index("samp")
-    tail = CHUNKS[1][0]
-    each = K_MAX // 4
-
-    def load(c):
-        rows = pl.ds(c * each, each)
-        return pltpu.make_async_copy(base_in.at[rows], base.at[rows], load_sem.at[c])
-
-    def store(c):
-        rows = pl.ds(c * each, each)
-        return pltpu.make_async_copy(fresh.at[rows], fitted.at[rows], out_sem.at[c])
-
-    for c in range(4):
-        load(c).start()
-    turned = resid[...].T
-    late = turned[:, tail:]
-    for g in range(DIST // 2):
-        part = jnp.dot(late, recent[:, g * 2 * SB:(g + 1) * 2 * SB], preferred_element_type=F32)
-        for j in range(ACT_DEV):
-            for side in range(2):
-                grad[j * DIST + g * 2 + side] = part[j * SB:(j + 1) * SB, side * SB:(side + 1) * SB]
-    for c in range(4):
-        load(c).wait()
-
-        @pl.loop(c * each, (c + 1) * each)
-        def _(k):
-            scale = RATE * tab[ROW_LIVE + k, samp].astype(F32)
-            fresh[k] = base[k] - scale * grad[tab[ROW_POS + k, samp]]
-
-        store(c).start()
-    resid_out[...] = jnp.dot(turned, sample_order(samp // 8), preferred_element_type=F32).astype(BF16)
-    for c in range(4):
-        store(c).wait()
 
 
 def per_device(slopes, targets, reconstructor, foot_act, foot_slope, foot_count):
     recon = reconstructor[0, 0]
     slopes = slopes.reshape(STEPS, LOCAL, SGB, SB).transpose(0, 2, 1, 3)
-    vmem, smem, anywhere = (pl.BlockSpec(memory_space=m) for m in (pltpu.VMEM, pltpu.SMEM, pl.ANY))
+    vmem = pl.BlockSpec(memory_space=pltpu.VMEM)
     grid_set = [pltpu.VMEM((SGB, LOCAL, SB), BF16)] * 5
     pick_set = [pltpu.VMEM((8, LOCAL, WIDE), BF16)] * 5
     far_set = [[pltpu.VMEM((8, LOCAL, WIDE), BF16)] * 2] * STEPS
     last_set = [[pltpu.VMEM((4, LOCAL, WIDE), BF16)] * 2] * STEPS
     dma = pltpu.SemaphoreType.DMA
     n_samp = foot_count.shape[1]
-    tail = SAMPLES - CHUNKS[1][0]
-    base, recent, resid, tab = pl.pallas_call(
+    fresh, fit_residual = pl.pallas_call(
         kernel,
         out_shape=(jax.ShapeDtypeStruct(recon.shape, F32),
-                   jax.ShapeDtypeStruct((tail, WIDE), BF16),
-                   jax.ShapeDtypeStruct((SAMPLES, ACT_DEV * SB), BF16),
-                   jax.ShapeDtypeStruct((TAB_ROWS, n_samp), jnp.int32)),
+                   jax.ShapeDtypeStruct((ACT_DEV * SB, SAMPLES), BF16)),
         in_specs=[pl.BlockSpec(memory_space=pltpu.HBM)] * 6,
-        out_specs=(anywhere, anywhere, vmem, anywhere),
+        out_specs=(vmem, vmem),
         scratch_shapes=[
             pltpu.VMEM(targets.shape, BF16),
             pltpu.VMEM((K_MAX, n_samp), jnp.int32),
@@ -470,39 +472,28 @@
             pltpu.VMEM((TAB_ROWS, n_samp), jnp.int32),
             pltpu.SMEM((TAB_ROWS, n_samp), jnp.int32),
             grid_set, grid_set, pick_set, pick_set,
-            far_set, far_set, last_set, last_set, [pltpu.VMEM((8, LOCAL, WIDE), BF16)] * STEPS,
+            far_set, far_set, last_set, last_set,
             pltpu.VMEM((8, 8, LOCAL, WIDE), BF16),
             pltpu.VMEM((8, 8, LOCAL, WIDE), BF16),
             pltpu.VMEM((STEPS, SAMPLES, WIDE), BF16),
             pltpu.VMEM((ACT_DEV * DIST, SB, SB), F32),
             pltpu.VMEM((WIDE, ACT_DEV * SB), BF16),
             pltpu.VMEM((K_MAX, SB, SB), F32),
-            pltpu.VMEM((K_MAX, SB, SB), F32),
+            pltpu.VMEM((ACT_DEV * DIST, SB, SB), F32),
+            pltpu.VMEM((SAMPLES, ACT_DEV * SB), BF16),
             pltpu.VMEM((STEPS, 4, SAMPLES, ACT_DEV * SB), BF16),
             pltpu.VMEM((STEPS, SAMPLES, ACT_DEV * SB), F32),
             pltpu.VMEM((SAMPLES, SAMPLES), BF16),
             dma((9,)),
             dma((2, STEPS, 4, 2)), dma((2, STEPS, 4, 2)),
             dma((STEPS, 8, 8)), dma((STEPS, 8, 8)),
-            dma((STEPS, 3, 3)), dma((STEPS, 3, 3)),
-            dma((2,)),
+            dma((STEPS, len(CHUNKS), 3)), dma((STEPS, len(CHUNKS), 3)),
         ],
         compiler_params=pltpu.CompilerParams(
             collective_id=0, has_side_effects=True, vmem_limit_bytes=40 * 1024 * 1024),
     )(*(pltpu.with_memory_space_constraint(x, pltpu.HBM) for x in (
         slopes, targets, recon, foot_act[0].T, foot_slope[0].T, foot_count)))
-    fitted, fit_residual = pl.pallas_call(
-        finish,
-        out_shape=(jax.ShapeDtypeStruct(recon.shape, F32),
-                   jax.ShapeDtypeStruct((ACT_DEV * SB, SAMPLES), BF16)),
-        in_specs=[anywhere, vmem, vmem, smem],
-        out_specs=(anywhere, vmem),
-        scratch_shapes=[pltpu.VMEM(recon.shape, F32), pltpu.VMEM(recon.shape, F32),
-                        pltpu.VMEM((ACT_DEV * DIST, SB, SB), F32),
-                        dma((4,)), dma((4,))],
-        compiler_params=pltpu.CompilerParams(vmem_limit_bytes=16 * 1024 * 1024),
-    )(base, recent, resid, tab)
-    return fitted[None, None], fit_residual
+    return fresh[None, None], fit_residual
 
 
 def solution(mesh):

time: 77.7 us -> 74.2 us (0.955)
  Pallas kernels: 76.9 us -> 71.5 us
  local copies, waits for them, and re-layouts: 0 us -> 1.98 us
    pallas_call x1 -> x0, Pallas kernels: 4.92 us -> none  [per_device(): pl.pallas_call(finish, out_shape=(jax.ShapeDtypeStruct(recon.shape, F32),...]
    unnamed x0 -> x2, local copies, waits for them, and re-layouts: none -> 1.98 us
where the time goes in v5:
time: 74.2 us; the launch traced here: 74.1 us
  Pallas kernels  71.5 us (96%)
  local copies, waits for them, and re-layouts  1.98 us (3%)
    pallas_call x1, Pallas kernels, per_device(): pl.pallas_call(kernel, out_shape=(jax.ShapeDtypeStruct(recon.shape, F32),...  71.5 us
    unnamed x2, local copies, waits for them, and re-layouts  1.98 us

profile of v5, /device:TPU:1, one launch (start us, length us, event | category | flops | bytes accessed | tf_op | source)
XLA Modules:
  0.0 74.1 jit_solution(12594841655377530825)
XLA Ops:
  0.6 71.5 %shard_map.77 = (f32[32,128,128]{2,1,0:T(8,128)S(1)}, bf16[256,256]{1,0:T(8,128)(2,1)S(1)}) custom-call(bf16[2,294,4,128]{3,2,1,0:T(4,128)(2,1)} %bitcast.13, bf16[2,256,256]{2,1,0:T(8,128)(2,1)} %targets_in.1, f32[32,128,128]{2,1,0:T(8,128)} %bitcast.12, s32[32,64]{1,0:T(8,128)} %bitcast.14, s32[32,64]{1,0:T(8,128)} %bitcast.15, s32[1,64]{1,0:T(1,128)} %count_in.1), custom_call_target="tpu_custom_call" | custom-call | tf_op jit(solution)/shard_map/pallas_call | solution.py:461
  72.1 1.3 %copy.10 = f32[1,1,32,128,128]{4,3,2,1,0:T(8,128)} copy(f32[1,1,32,128,128]{4,3,2,1,0:T(8,128)S(1)} %bitcast.11) | data formatting | bytes 4194304
  73.4 0.7 copy.11

commit v6 on v5

--- a/solution.py
+++ b/solution.py
@@ -28,7 +28,7 @@
     return OFFS.index(4 if off == -4 else off)
 
 
-CHUNKS = ((0, 96), (96, 160), (160, 224), (224, 256))
+CHUNKS = ((0, 96), (96, 160), (160, 256))
 ROW_POS = 24
 ROW_SLOT = ROW_POS + K_MAX
 ROW_MASK = ROW_SLOT + ACT_DEV * DIST
@@ -76,7 +76,7 @@
 
 
 def kernel(slopes, targets_in, recon, act_in, slope_in, count_in, fresh, resid_out,
-           targets, act, slope, count, tab_v, tab, grid0, grid1, pick0, pick1, far_out, far_in, last_out, last_mid,
+           targets, act, slope, count, tab_v, tab, grid0, grid1, pick0, pick1, far_out, last_out, last_mid,
            got0, got1, mat, weights, low_t, recon_v, grad_v, resid,
            preds, goal, perm, load_sem, zs, zr, xs, xr, ys, yr):
     grids, picks, gots = (grid0, grid1), (pick0, pick1), (got0, got1)
@@ -105,14 +105,23 @@
             device_id_type=MESH,
         )
 
-    def far_copy(way, t, half):
-        rows = pl.ds(half * 4, 4)
-        return pltpu.make_async_remote_copy(
-            src_ref=far_out[t][way].at[rows],
-            dst_ref=far_in[t][way].at[rows],
-            send_sem=zs.at[way, t, 2, half],
-            recv_sem=zr.at[way, t, 2, half],
-            device_id=z_dev(1 - 2 * way),
+    def far_copy(way, t, q):
+        return pltpu.make_async_remote_copy(
+            src_ref=far_out[t][way].at[q],
+            dst_ref=gots[t].at[5 + way, own_q],
+            send_sem=xs.at[t, 5 + way, q],
+            recv_sem=xr.at[t, 5 + way, own_q],
+            device_id=(sens, (plane + 1 - 2 * way + 8) % 8 * 8 + q),
+            device_id_type=MESH,
+        )
+
+    def far_arrival(way, t, q):
+        return pltpu.make_async_remote_copy(
+            src_ref=far_out[t][way].at[q],
+            dst_ref=gots[t].at[5 + way, q],
+            send_sem=xs.at[t, 5 + way, q],
+            recv_sem=xr.at[t, 5 + way, q],
+            device_id=(sens, (plane - 1 + 2 * way + 8) % 8 * 8 + q),
             device_id_type=MESH,
         )
 
@@ -147,14 +156,9 @@
             device_id_type=MESH,
         )
 
-    def x_source(t, r, e):
-        if r < 5:
-            return picks[t][r].at[e]
-        return far_in[t][r - 5].at[q_of(e, 1)]
-
     def x_copy(t, r, e):
         return pltpu.make_async_remote_copy(
-            src_ref=x_source(t, r, e),
+            src_ref=picks[t][r].at[e],
             dst_ref=gots[t].at[r, own_q],
             send_sem=xs.at[t, r, e],
             recv_sem=xr.at[t, r, e],
@@ -164,7 +168,7 @@
 
     def x_arrival(t, r, e):
         return pltpu.make_async_remote_copy(
-            src_ref=x_source(t, r, e),
+            src_ref=picks[t][r].at[e],
             dst_ref=gots[t].at[r, q_of(e, -1)],
             send_sem=xs.at[t, r, e],
             recv_sem=xr.at[t, r, e],
@@ -211,8 +215,11 @@
         def _(e):
             pick_one(grids[t][r], plane * 8 + q_of(e, 1), picks[t][r].at[e])
 
-        for e in range(1, 8):
-            x_copy(t, r, e).start()
+            @pl.when(e > 1)
+            def _():
+                x_copy(t, r, e - 1).start()
+
+        x_copy(t, r, 7).start()
 
     def pick_far(t):
         for half in range(2):
@@ -226,40 +233,33 @@
                 pick_one(grids[t][3 + way], ahead + q, last_out[t][way].at[q])
 
             mid_copy(way, t).start()
-        for half in range(2):
+        near = [(plane + 1 - 2 * way + 8) % 8 * 8 for way in range(2)]
+
+        @pl.loop(0, 8)
+        def _(i):
             for way in range(2):
-                ahead = (plane + 1 - 2 * way + 8) % 8 * 8
-
-                @pl.loop(half * 4, half * 4 + 4)
-                def _(q):
-                    pick_one(grids[t][3 + way], ahead + q, far_out[t][way].at[q])
-
-                far_copy(way, t, half).start()
+                q = (own_q + i) % 8
+                pick_one(grids[t][3 + way], near[way] + q, far_out[t][way].at[q])
+
+                @pl.when(i > 0)
+                def _():
+                    far_copy(way, t, (own_q + i + 7) % 8).start()
+
+        for way in range(2):
+            far_copy(way, t, (own_q + 7) % 8).start()
 
     def pass_last(t):
         for way in range(2):
             mid_copy(way, t).wait_recv()
             for i in range(4):
-                last_copy(way, t, i).start()
-
-    def relay_far(t, half):
-        for way in range(2):
-            far_copy(way, t, half).wait_recv()
-            for q in range(half * 4, half * 4 + 4):
-                e = ((q // 2 - col + 4) % 4) * 2 + (q + core) % 2
-
-                @pl.when(own_q != q)
-                def _():
-                    x_copy(t, 5 + way, e).start()
-
-            @pl.when(own_q // 4 == half)
-            def _():
-                gots[t][5 + way, own_q] = far_in[t][way][own_q]
+                last_copy(way, t, (own_q + i) % 4).start()
 
     def assemble(t, r):
         for e in range(8):
             if r == 7:
                 last_arrival(t, e).wait_recv()
+            elif r > 4:
+                far_arrival(r - 5, t, e).wait_recv()
             elif e > 0:
                 x_arrival(t, r, e).wait_recv()
         for half in range(2):
@@ -317,16 +317,14 @@
     recon_load.start()
 
     barrier = pltpu.get_barrier_semaphore()
-    for step in (1, -1):
-        pl.semaphore_signal(barrier, inc=1, device_id=z_dev(step), device_id_type=MESH)
     for e in range(1, 8):
         pl.semaphore_signal(barrier, inc=1, device_id=(sens, plane * 8 + q_of(e, 1)), device_id_type=MESH)
     for e in range(1, 4):
         pl.semaphore_signal(barrier, inc=1, device_id=((sens + e) % 4, samp), device_id_type=MESH)
-    for q in range(8):
-        back = (plane - 1 + 2 * (own_q // 4) + 8) % 8
-        pl.semaphore_signal(barrier, inc=1, device_id=(sens, back * 8 + q), device_id_type=MESH)
-    pl.semaphore_wait(barrier, 20)
+    for step in (1, 7):
+        for q in range(8):
+            pl.semaphore_signal(barrier, inc=1, device_id=(sens, (plane + step) % 8 * 8 + q), device_id_type=MESH)
+    pl.semaphore_wait(barrier, 26)
 
     own_loads[0].wait()
     for half in range(2):
@@ -359,64 +357,55 @@
         z_copy(way, 1, 0, 0).start()
     pick(0, 1)
     pick(0, 2)
-    assemble(0, 0)
     pick_far(0)
     pick(0, 3)
     pick(0, 4)
-    assemble(0, 1)
-    assemble(0, 2)
-    predict(0, 0)
     pass_last(0)
     for way in range(2):
         z_copy(way, 1, 0, 1).start()
     forward(1, 0)
     pick(1, 0)
-    relay_far(0, 0)
+    for r in range(3):
+        assemble(0, r)
+    predict(0, 0)
+    forward(1, 1)
+    pick(1, 1)
+    pick(1, 2)
     assemble(0, 3)
     assemble(0, 4)
     predict(0, 1)
-    relay_far(0, 1)
-    residual(0, 0)
-    assemble(0, 5)
-    assemble(0, 6)
+    for r in range(5, 8):
+        assemble(0, r)
     predict(0, 2)
-    forward(1, 1)
-    assemble(0, 7)
-    predict(0, 3)
-    pick(1, 1)
-    pick(1, 2)
     pick_far(1)
     pick(1, 3)
     pick(1, 4)
-    assemble(1, 0)
-    for c in range(1, 4):
+    for c in range(3):
         residual(0, c)
     gradient(0, 0, SAMPLES)
     pass_last(1)
-    assemble(1, 1)
-    assemble(1, 2)
+    for r in range(3):
+        assemble(1, r)
     predict(1, 0)
-    relay_far(1, 0)
-    relay_far(1, 1)
     assemble(1, 3)
     assemble(1, 4)
     predict(1, 1)
     assemble(1, 5)
     assemble(1, 6)
+    assemble(1, 7)
     predict(1, 2)
-    assemble(1, 7)
-    predict(1, 3)
-    tail = CHUNKS[3][0]
-    for c in range(3):
+    tail = CHUNKS[2][0]
+    for c in range(2):
         residual(1, c)
     gradient(1, 0, tail)
 
-    @pl.loop(0, K_MAX)
-    def _(k):
-        live = tab[ROW_LIVE + k, samp].astype(F32)
-        fresh[k] = weights[tab[ROW_POS + k, samp]] * live + recon_v[k] * (1.0 - live)
-
-    residual(1, 3)
+    @pl.loop(0, K_MAX // 4)
+    def _(i):
+        for k in (i * 4, i * 4 + 1, i * 4 + 2, i * 4 + 3):
+            live = tab[ROW_LIVE + k, samp].astype(F32)
+            fresh[k] = weights[tab[ROW_POS + k, samp]] * live + recon_v[k] * (1.0 - live)
+
+    residual(1, 2)
     turned = resid[...].T
     late = turned[:, tail:]
     for g in range(DIST // 2):
@@ -426,21 +415,23 @@
                 grad_v[j * DIST + g * 2 + side] = part[j * SB:(j + 1) * SB, side * SB:(side + 1) * SB]
     resid_out[...] = jnp.dot(turned, perm[...], preferred_element_type=F32).astype(BF16)
 
-    @pl.loop(0, K_MAX)
-    def _(k):
-        scale = RATE * tab[ROW_LIVE + k, samp].astype(F32)
-        fresh[k] = fresh[k] - scale * grad_v[tab[ROW_POS + k, samp]]
+    @pl.loop(0, K_MAX // 4)
+    def _(i):
+        for k in (i * 4, i * 4 + 1, i * 4 + 2, i * 4 + 3):
+            scale = RATE * tab[ROW_LIVE + k, samp].astype(F32)
+            fresh[k] = fresh[k] - scale * grad_v[tab[ROW_POS + k, samp]]
 
     for t in range(STEPS):
         for way in range(2):
             for half in range(2):
                 for hop in range(2):
                     z_copy(way, t, hop, half).wait_send()
-                far_copy(way, t, half).wait_send()
             mid_copy(way, t).wait_send()
+            for q in range(8):
+                far_copy(way, t, q).wait_send()
             for i in range(4):
                 last_copy(way, t, i).wait_send()
-        for r in range(7):
+        for r in range(5):
             for e in range(1, 8):
                 x_copy(t, r, e).wait_send()
         for c in range(len(CHUNKS)):
@@ -472,7 +463,7 @@
             pltpu.VMEM((TAB_ROWS, n_samp), jnp.int32),
             pltpu.SMEM((TAB_ROWS, n_samp), jnp.int32),
             grid_set, grid_set, pick_set, pick_set,
-            far_set, far_set, last_set, last_set,
+            far_set, last_set, last_set,
             pltpu.VMEM((8, 8, LOCAL, WIDE), BF16),
             pltpu.VMEM((8, 8, LOCAL, WIDE), BF16),
             pltpu.VMEM((STEPS, SAMPLES, WIDE), BF16),

time: 74.2 us -> 70.3 us (0.947)
  Pallas kernels: 71.5 us -> 67.6 us
    pallas_call x1, Pallas kernels: 71.5 us -> 67.6 us  [per_device(): pl.pallas_call(kernel, out_shape=(jax.ShapeDtypeStruct(recon.shape, F32),...]
where the time goes in v6:
time: 70.3 us
  Pallas kernels  67.6 us (96%)
  local copies, waits for them, and re-layouts  1.98 us (3%)
    pallas_call x1, Pallas kernels, per_device(): pl.pallas_call(kernel, out_shape=(jax.ShapeDtypeStruct(recon.shape, F32),...  67.6 us
    unnamed x2, local copies, waits for them, and re-layouts  1.98 us

profile of v6, /device:TPU:1, one launch (start us, length us, event | category | flops | bytes accessed | tf_op | source)
XLA Modules:
  0.0 70.3 jit_solution(5823441242481011409)
XLA Ops:
  0.6 67.6 %shard_map.77 = (f32[32,128,128]{2,1,0:T(8,128)S(1)}, bf16[256,256]{1,0:T(8,128)(2,1)S(1)}) custom-call(bf16[2,294,4,128]{3,2,1,0:T(4,128)(2,1)} %bitcast.13, bf16[2,256,256]{2,1,0:T(8,128)(2,1)} %targets_in.1, f32[32,128,128]{2,1,0:T(8,128)} %bitcast.12, s32[32,64]{1,0:T(8,128)} %bitcast.14, s32[32,64]{1,0:T(8,128)} %bitcast.15, s32[1,64]{1,0:T(1,128)} %count_in.1), custom_call_target="tpu_custom_call" | custom-call | tf_op jit(solution)/shard_map/pallas_call | solution.py:452
  68.3 1.3 %copy.10 = f32[1,1,32,128,128]{4,3,2,1,0:T(8,128)} copy(f32[1,1,32,128,128]{4,3,2,1,0:T(8,128)S(1)} %bitcast.11) | data formatting | bytes 4194304
  69.6 0.7 copy.11

commit v7 on v6

--- a/solution.py
+++ b/solution.py
@@ -277,7 +277,7 @@
         rows = slice(*CHUNKS[c])
         part = jnp.dot(mat[t, rows], low_t[...], preferred_element_type=F32)
         preds[t, sens, rows] = part.astype(BF16)
-        for e in range(1, 4):
+        for e in (2, 1, 3):
             y_copy(t, c, e).start()
 
     def residual(t, c):

time: 70.3 us -> 70.3 us (level)
  no operation moved by 1% of the time
where the time goes in v7:
time: 70.3 us; the launch traced here: 70.2 us
  Pallas kernels  67.6 us (96%)
  local copies, waits for them, and re-layouts  1.98 us (3%)
    pallas_call x1, Pallas kernels, per_device(): pl.pallas_call(kernel, out_shape=(jax.ShapeDtypeStruct(recon.shape, F32),...  67.6 us
    unnamed x2, local copies, waits for them, and re-layouts  1.98 us

profile of v7, /device:TPU:1, one launch (start us, length us, event | category | flops | bytes accessed | tf_op | source)
XLA Modules:
  0.0 70.2 jit_solution(2660285760819933940)
XLA Ops:
  0.6 67.6 %shard_map.77 = (f32[32,128,128]{2,1,0:T(8,128)S(1)}, bf16[256,256]{1,0:T(8,128)(2,1)S(1)}) custom-call(bf16[2,294,4,128]{3,2,1,0:T(4,128)(2,1)} %bitcast.13, bf16[2,256,256]{2,1,0:T(8,128)(2,1)} %targets_in.1, f32[32,128,128]{2,1,0:T(8,128)} %bitcast.12, s32[32,64]{1,0:T(8,128)} %bitcast.14, s32[32,64]{1,0:T(8,128)} %bitcast.15, s32[1,64]{1,0:T(1,128)} %count_in.1), custom_call_target="tpu_custom_call" | custom-call | tf_op jit(solution)/shard_map/pallas_call | solution.py:452
  68.2 1.3 %copy.10 = f32[1,1,32,128,128]{4,3,2,1,0:T(8,128)} copy(f32[1,1,32,128,128]{4,3,2,1,0:T(8,128)S(1)} %bitcast.11) | data formatting | bytes 4194304
  69.5 0.7 copy.11
